TPU v7x, 128 devices: a whole 4x4x4 slice. The times are simulated.
128 devices in a mesh: box: 16 (over x, y_lo, core), depth: 8 (over y_hi, z).
Axes of the slice: x: 4, y: 4 (y_hi: 2, y_lo: 2; y = y_hi * 2 + y_lo), z: 4, core: 2. Of those that a mesh axis runs over, the one named last changes fastest.
Arguments:
- positions: float32 [3, 16384, 128], P(None, ('box', 'depth')), may hold values from -0.5 to 0.5
- charges: float32 [2, 16384, 128], P(None, ('box', 'depth')), may hold values from -0.8 to 0.8
- counts: int32 [16384], P(('box', 'depth')), may hold values from 1 to 128
- owners: int32 [16384, 1], P(('box', 'depth')), may hold values from 0 to 127; in each aligned block of 128 rows (0 to 127, 128 to 255, ...) at most 2 rows name the same one
- leaves: int32 [16384], P(('box', 'depth')), may hold values from 0 to 255
- near_lists: int32 [64, 8, 4096], P(None, 'depth', 'box'), may hold values from 0 to 767
- image_lists: int32 [64, 8, 4096], P(None, 'depth', 'box'), may hold values from 0 to 767
- upward: float32 [304, 304], replicated, may hold values from -0.3125 to 0.3125
- child_ops: bfloat16 [304, 2432], replicated, may hold values from -0.125 to 0.125
- direct_ops: bfloat16 [19456, 304], replicated, may hold values from -0.0390625 to 0.0390625
- image_ops: bfloat16 [19456, 304], replicated, may hold values from -0.0390625 to 0.0390625
Outputs:
- potentials: float32 [304, 8, 4096], P(None, 'depth', 'box')
- parents: float32 [304, 8, 512], P(None, 'depth', 'box')
Inputs may be any that keep to these rules, and one draw needn't show every extreme that they name: `owners`: no device's 128 blocks name one owner more than 2 times, and some device's blocks name some owner exactly 2 times.
All inputs are finite; a program needn't handle non-finite values.
Results may differ from a plain program's by a relative error of at most 0.0029.
Values may be sent and summed in bfloat16 or wider, within the bound.
A program may use at most 128 MiB of HBM per device.

v0:
```python
import math

import jax
import jax.numpy as jnp
import numpy as np
from jax import lax
from jax.sharding import PartitionSpec as P

GRID = 6


wavenumber = 2.0


def extended(cells, sides, width):
    for axis, dim in sides:
        count = lax.axis_size(axis)
        ends = count - 1
        head = lax.slice_in_dim(cells, 0, width, axis=dim)
        tail = lax.slice_in_dim(cells, cells.shape[dim] - width, cells.shape[dim], axis=dim)
        cells = jnp.concatenate(
            [
                lax.ppermute(tail, axis, [(i, (i + 1) % count) for i in range(ends)]),
                cells,
                lax.ppermute(head, axis, [((i + 1) % count, i) for i in range(ends)]),
            ],
            axis=dim,
        )
    return cells


def swapped(block, axis, stride):
    count = lax.axis_size(axis)
    route = []
    for low in range(count):
        high = low | 1 << stride
        if high != low and high < count:
            route += [(low, high), (high, low)]
    return lax.ppermute(block, axis, route)


def surface_points(grid_size):
    indices = np.arange(grid_size)
    lattice = np.stack(np.meshgrid(indices, indices, indices, indexing="ij"), -1).reshape(-1, 3)
    outside = np.any((lattice == 0) | (lattice == grid_size - 1), axis=1)
    middle = (grid_size - 1) / 2.0
    return ((lattice[outside] - middle) * (1.5 / middle)).astype(np.float32)


def block_check(positions, charges):
    points = jnp.asarray(surface_points(GRID))
    delta_x = points[:, 0][:, None, None] - positions[0][None]
    delta_y = points[:, 1][:, None, None] - positions[1][None]
    delta_z = points[:, 2][:, None, None] - positions[2][None]
    radius = jnp.sqrt(delta_x * delta_x + delta_y * delta_y + delta_z * delta_z)
    cosine = jnp.cos(wavenumber * radius) / radius
    sine_part = jnp.sin(wavenumber * radius) / radius
    real_part = jnp.sum(cosine * charges[0][None] - sine_part * charges[1][None], axis=2)
    imaginary = jnp.sum(sine_part * charges[0][None] + cosine * charges[1][None], axis=2)
    return jnp.concatenate([real_part, imaginary], axis=0)


def checks_by_group(positions, charges):
    blocks = positions.shape[1]
    group_size = math.gcd(blocks, 32)
    group_count = blocks // group_size
    place_groups = positions.reshape(3, group_count, group_size, positions.shape[2]).transpose(
        1, 0, 2, 3
    )
    charge_groups = charges.reshape(2, group_count, group_size, charges.shape[2]).transpose(
        1, 0, 2, 3
    )

    def one_group(grouped):
        return block_check(grouped[0], grouped[1])

    values = lax.map(one_group, (place_groups, charge_groups))
    return values.transpose(1, 0, 2).reshape(values.shape[1], blocks)


def deliver(payload, leaf_row):
    return (
        lax.all_to_all(payload, ("box", "depth"), split_axis=1, concat_axis=1, tiled=True),
        lax.all_to_all(leaf_row, ("box", "depth"), split_axis=1, concat_axis=1, tiled=True),
    )


def translate(operators, window, lists):
    window_rows = window.T
    picked = lists[:, 0, :].T
    gathered = jnp.take(window_rows, picked, axis=0)
    flat = gathered.reshape(gathered.shape[0], -1)
    return jnp.dot(flat, operators, preferred_element_type=jnp.float32)


def local(
    positions,
    charges,
    counts,
    owners,
    leaves,
    near_lists,
    image_lists,
    upward,
    child_ops,
    direct_ops,
    image_ops,
):
    box_count = lax.axis_size("box")
    depth_count = lax.axis_size("depth")
    devices = box_count * depth_count
    blocks = positions.shape[1]
    row_count = positions.shape[2]
    capacity = 2 * blocks // devices
    slots = devices * capacity
    leaf_count = near_lists.shape[2]
    live = (jnp.arange(row_count, dtype=jnp.int32)[None, :] < counts[:, None]).astype(jnp.float32)
    masked = charges * live[None]
    target = owners[:, 0]
    order = jnp.arange(blocks, dtype=jnp.int32)
    earlier = (target[:, None] == target[None, :]) & (order[None, :] < order[:, None])
    slot_index = target * capacity + jnp.sum(earlier.astype(jnp.int32), axis=1)
    leaf_row = (
        jnp.full((1, slots), -1.0, jnp.float32).at[0, slot_index].set(leaves.astype(jnp.float32))
    )
    stacked = jnp.concatenate([positions, masked], axis=0)
    payload = jnp.zeros((5, slots, row_count), jnp.float32).at[:, slot_index, :].set(stacked)
    arrived, arrived_leaf = deliver(payload, leaf_row)
    block_values = checks_by_group(arrived[:3], arrived[3:])
    members = (
        arrived_leaf[0][:, None] == jnp.arange(leaf_count, dtype=jnp.float32)[None, :]
    ).astype(jnp.float32)
    check = jnp.dot(block_values, members, precision=lax.Precision.HIGHEST)
    multipole = jnp.dot(upward, check, precision=lax.Precision.HIGHEST).astype(jnp.bfloat16)
    channels = multipole.shape[0]
    children = (
        multipole.reshape(channels, leaf_count // 8, 8)
        .transpose(0, 2, 1)
        .reshape(channels * 8, leaf_count // 8)
    )
    parents = jnp.dot(child_ops, children, preferred_element_type=jnp.float32)
    window = extended(multipole, (("box", 1),), leaf_count)
    direct = translate(direct_ops, window, near_lists)
    bit_total = depth_count.bit_length() - 1
    mirrored = multipole
    for bit_number in range(bit_total):
        mirrored = swapped(mirrored, "depth", bit_number)
    image_window = extended(mirrored, (("box", 1),), leaf_count)
    reflected = translate(image_ops, image_window, image_lists)
    return ((direct + reflected).T[:, None, :], parents[:, None, :])


def solution(mesh):
    return jax.shard_map(
        local,
        mesh=mesh,
        in_specs=(
            P(None, ("box", "depth"), None),
            P(None, ("box", "depth"), None),
            P(("box", "depth")),
            P(("box", "depth"), None),
            P(("box", "depth")),
            P(None, "depth", "box"),
            P(None, "depth", "box"),
            P(),
            P(),
            P(),
            P(),
        ),
        out_specs=(P(None, "depth", "box"), P(None, "depth", "box")),
        check_vma=False,
    )
```

profile of v0, /device:TPU:1, one launch (start us, length us, event | category | flops | bytes accessed | tf_op | source)
XLA Modules:
  0.0 390.7 jit_solution(15532718104468842067)
XLA Ops:
  0.7 1.0 convert_reduce_fusion
  1.6 0.7 fusion.8
  2.3 0.7 convert_element_type.22
  3.0 1.0 scatter_custom_fusion.1
  3.9 0.8 all_to_all.10
  4.7 11.5 %all-to-all-start.1 = ((f32[1,128,2]{2,0,1:T(1,128)}), f32[1,128,2]{2,0,1:T(1,128)S(1)}, u32[]{:S(2)}, u32[]{:S(2)}) async-start(f32[1,128,2]{2,0,1:T(1,128)} %bitcast.11), calls=%async_computation.1 | async-start | bytes 131072 | tf_op jit(solution)/shard_map/all_to_all | solution.py:84
  16.2 0.7 fusion.7
  17.0 0.9 compare_select_fusion.1
  17.8 0.1 copy.54
  17.9 0.1 reshape.114
  18.1 0.9 compare_select_fusion
  18.9 0.9 broadcast_multiply_fusion
  19.9 1.0 maximum_bitcast_fusion.3
  20.8 0.2 copy.50
  21.0 0.1 copy.57
  21.2 1.0 broadcast_in_dim.38
  22.3 12.4 %scatter_fusion = f32[5,256,128]{2,0,1:T(8,128)} fusion(f32[5,256,128]{2,0,1:T(8,128)} %broadcast_in_dim.38, s32[128]{0:T(128)S(1)} %fusion.8, f32[128,5,128]{2,1,0:T(8,128)S(1)} %copy.50), kind=kCustom, calls=%fused_computation.2 | custom fusion | bytes 983552 | tf_op jit(solution)/shard_map/scatter | solution.py:127
  34.6 9.8 %all-to-all-start = ((f32[5,256,128]{2,0,1:T(8,128)}), f32[5,256,128]{2,0,1:T(8,128)S(1)}, u32[]{:S(2)}, u32[]{:S(2)}) async-start(f32[5,256,128]{2,0,1:T(8,128)} %scatter_fusion), calls=%async_computation | async-start | bytes 2097152 | tf_op jit(solution)/shard_map/all_to_all | solution.py:83
  44.5 0.5 broadcast.64
  45.0 0.8 reduce.3
  45.8 0.1 eq.34
  46.0 17.4 %all-to-all-done = f32[5,256,128]{2,0,1:T(8,128)S(1)} async-done(((f32[5,256,128]{2,0,1:T(8,128)}), f32[5,256,128]{2,0,1:T(8,128)S(1)}, u32[]{:S(2)}, u32[]{:S(2)}) %all-to-all-start) | async-done | bytes 655392 | tf_op jit(solution)/shard_map/all_to_all | solution.py:83
  63.3 0.1 slice.61
  63.5 0.1 slice.62
  63.7 108.3 %while.11 = (s32[]{:T(128)}, f32[8,304,32]{1,2,0:T(8,128)}, f32[8,3,32,128]{3,2,1,0:T(8,128)S(1)}, f32[8,2,32,128]{3,2,1,0:T(8,128)S(1)}, s32[]{:T(128)}, /*inde...) while((s32[]{:T(128)}, f32[8,304,32]{1,2,0:T(8,128)}, ...), condition=%wide.region_5.6_spmd.clone, body=%wide.region_2.5_spmd.sunk.clone.sunk | while | flops 11829252 | bytes 452541 | solution.py:77
  63.7 12.7 %subtract_reduce_fusion.2 = (f32[152,32]{1,0:T(8,128)S(1)}, f32[152,32]{1,0:T(8,128)S(1)}) fusion(f32[32,128]{1,0:T(8,128)S(1)} %get-tuple-element.104, f32[32,128]{1,0:T(8,128)S(1)} %get-tuple-element.105, f32[32,128]{1,0:T(8,128)S(1)} %get-tuple-element.106, f32[152]{0:T(256)S(1)} %get-tuple-element.141, f32[32,128]{1,0:T(8,128)S(1)} %get-tuple-element.107, ...), kind=kLoop, calls=%fused_computation.5.clone.1 | loop fusion | flops 11819520 | bytes 122656 | tf_op jit(solution)/shard_map/while/body/eval_jaxpr/reduce_sum | solution.py:58
  76.6 0.7 fusion.21
  77.3 12.7 %subtract_reduce_fusion.2 = (f32[152,32]{1,0:T(8,128)S(1)}, f32[152,32]{1,0:T(8,128)S(1)}) fusion(f32[32,128]{1,0:T(8,128)S(1)} %get-tuple-element.104, f32[32,128]{1,0:T(8,128)S(1)} %get-tuple-element.105, f32[32,128]{1,0:T(8,128)S(1)} %get-tuple-element.106, f32[152]{0:T(256)S(1)} %get-tuple-element.141, f32[32,128]{1,0:T(8,128)S(1)} %get-tuple-element.107, ...), kind=kLoop, calls=%fused_computation.5.clone.1 | loop fusion | flops 11819520 | bytes 122656 | tf_op jit(solution)/shard_map/while/body/eval_jaxpr/reduce_sum | solution.py:58
  90.1 0.7 fusion.21
  90.8 12.7 %subtract_reduce_fusion.2 = (f32[152,32]{1,0:T(8,128)S(1)}, f32[152,32]{1,0:T(8,128)S(1)}) fusion(f32[32,128]{1,0:T(8,128)S(1)} %get-tuple-element.104, f32[32,128]{1,0:T(8,128)S(1)} %get-tuple-element.105, f32[32,128]{1,0:T(8,128)S(1)} %get-tuple-element.106, f32[152]{0:T(256)S(1)} %get-tuple-element.141, f32[32,128]{1,0:T(8,128)S(1)} %get-tuple-element.107, ...), kind=kLoop, calls=%fused_computation.5.clone.1 | loop fusion | flops 11819520 | bytes 122656 | tf_op jit(solution)/shard_map/while/body/eval_jaxpr/reduce_sum | solution.py:58
  103.6 0.7 fusion.21
  104.4 12.7 %subtract_reduce_fusion.2 = (f32[152,32]{1,0:T(8,128)S(1)}, f32[152,32]{1,0:T(8,128)S(1)}) fusion(f32[32,128]{1,0:T(8,128)S(1)} %get-tuple-element.104, f32[32,128]{1,0:T(8,128)S(1)} %get-tuple-element.105, f32[32,128]{1,0:T(8,128)S(1)} %get-tuple-element.106, f32[152]{0:T(256)S(1)} %get-tuple-element.141, f32[32,128]{1,0:T(8,128)S(1)} %get-tuple-element.107, ...), kind=kLoop, calls=%fused_computation.5.clone.1 | loop fusion | flops 11819520 | bytes 122656 | tf_op jit(solution)/shard_map/while/body/eval_jaxpr/reduce_sum | solution.py:58
  117.2 0.7 fusion.21
  117.9 12.7 %subtract_reduce_fusion.2 = (f32[152,32]{1,0:T(8,128)S(1)}, f32[152,32]{1,0:T(8,128)S(1)}) fusion(f32[32,128]{1,0:T(8,128)S(1)} %get-tuple-element.104, f32[32,128]{1,0:T(8,128)S(1)} %get-tuple-element.105, f32[32,128]{1,0:T(8,128)S(1)} %get-tuple-element.106, f32[152]{0:T(256)S(1)} %get-tuple-element.141, f32[32,128]{1,0:T(8,128)S(1)} %get-tuple-element.107, ...), kind=kLoop, calls=%fused_computation.5.clone.1 | loop fusion | flops 11819520 | bytes 122656 | tf_op jit(solution)/shard_map/while/body/eval_jaxpr/reduce_sum | solution.py:58
  130.7 0.7 fusion.21
  131.4 12.7 %subtract_reduce_fusion.2 = (f32[152,32]{1,0:T(8,128)S(1)}, f32[152,32]{1,0:T(8,128)S(1)}) fusion(f32[32,128]{1,0:T(8,128)S(1)} %get-tuple-element.104, f32[32,128]{1,0:T(8,128)S(1)} %get-tuple-element.105, f32[32,128]{1,0:T(8,128)S(1)} %get-tuple-element.106, f32[152]{0:T(256)S(1)} %get-tuple-element.141, f32[32,128]{1,0:T(8,128)S(1)} %get-tuple-element.107, ...), kind=kLoop, calls=%fused_computation.5.clone.1 | loop fusion | flops 11819520 | bytes 122656 | tf_op jit(solution)/shard_map/while/body/eval_jaxpr/reduce_sum | solution.py:58
  144.2 0.7 fusion.21
  144.9 12.7 %subtract_reduce_fusion.2 = (f32[152,32]{1,0:T(8,128)S(1)}, f32[152,32]{1,0:T(8,128)S(1)}) fusion(f32[32,128]{1,0:T(8,128)S(1)} %get-tuple-element.104, f32[32,128]{1,0:T(8,128)S(1)} %get-tuple-element.105, f32[32,128]{1,0:T(8,128)S(1)} %get-tuple-element.106, f32[152]{0:T(256)S(1)} %get-tuple-element.141, f32[32,128]{1,0:T(8,128)S(1)} %get-tuple-element.107, ...), kind=kLoop, calls=%fused_computation.5.clone.1 | loop fusion | flops 11819520 | bytes 122656 | tf_op jit(solution)/shard_map/while/body/eval_jaxpr/reduce_sum | solution.py:58
  157.8 0.7 fusion.21
  158.5 12.7 %subtract_reduce_fusion.2 = (f32[152,32]{1,0:T(8,128)S(1)}, f32[152,32]{1,0:T(8,128)S(1)}) fusion(f32[32,128]{1,0:T(8,128)S(1)} %get-tuple-element.104, f32[32,128]{1,0:T(8,128)S(1)} %get-tuple-element.105, f32[32,128]{1,0:T(8,128)S(1)} %get-tuple-element.106, f32[152]{0:T(256)S(1)} %get-tuple-element.141, f32[32,128]{1,0:T(8,128)S(1)} %get-tuple-element.107, ...), kind=kLoop, calls=%fused_computation.5.clone.1 | loop fusion | flops 11819520 | bytes 122656 | tf_op jit(solution)/shard_map/while/body/eval_jaxpr/reduce_sum | solution.py:58
  171.3 0.7 fusion.21
  172.0 1.5 fusion.4
  173.5 0.7 fusion.2
  174.2 0.6 collective-permute-start.2
  174.9 3.6 collective-permute-start.1
  178.5 2.0 collective-permute-start
  180.5 0.2 copy.60
  180.6 0.5 copy.61
  181.1 1.7 collective-permute-start.3
  182.8 1.2 convolution_bitcast_fusion
  184.0 0.3 copy.55
  184.3 65.6 %gather_fusion = bf16[16384,304]{1,0:T(8,128)(2,1)} fusion(bf16[768,304]{1,0:T(8,128)(2,1)S(1)} %copy.55, s32[16384]{0:T(1024)S(1)} %broadcast_clamp_fusion.1), kind=kCustom, calls=%fused_computation.clone | custom fusion | bytes 19988480 | tf_op jit(solution)/shard_map/jit(_take)/gather | solution.py:91
  249.9 15.8 %copy.56 = bf16[256,64,304]{0,2,1:T(8,128)(2,1)} copy(bf16[256,64,304]{2,1,0:T(8,128)(2,1)} %bitcast.84) | data formatting | bytes 19922944 | tf_op jit(solution)/shard_map/jit(_take)/gather | solution.py:91
  265.6 0.7 collective-permute-start.4
  266.3 8.5 %broadcast_select_fusion.1 = bf16[256,64,304]{0,2,1:T(8,128)(2,1)} fusion(bf16[256,64,304]{0,2,1:T(8,128)(2,1)} %copy.56, pred[256,64]{0,1:T(8,128)(4,1)S(1)} %compare_and_fusion.1), kind=kLoop, calls=%fused_computation.17 | loop fusion | flops 4980736 | bytes 19939328 | tf_op jit(solution)/shard_map/jit(_take)/select_n | solution.py:91
  274.9 2.4 collective-permute-start.6
  277.2 3.7 collective-permute-start.5
  280.9 9.2 %fusion.11 = f32[256,304]{0,1:T(8,128)S(1)} fusion(bf16[19456,304]{0,1:T(8,128)(2,1)} %param.25, bf16[256,19456]{0,1:T(8,128)(2,1)} %bitcast.86), kind=kOutput, calls=%fused_computation.49 | convolution fusion | flops 3028287488 | bytes 22102016 | tf_op jit(solution)/shard_map/dot_general | solution.py:93
  290.2 0.3 copy.58
  290.5 65.6 %gather_fusion.1 = bf16[16384,304]{1,0:T(8,128)(2,1)} fusion(bf16[768,304]{1,0:T(8,128)(2,1)S(1)} %copy.58, s32[16384]{0:T(1024)S(1)} %broadcast_clamp_fusion), kind=kCustom, calls=%fused_computation.1.clone | custom fusion | bytes 19988480 | tf_op jit(solution)/shard_map/jit(_take)/gather | solution.py:91
  356.1 15.8 %copy.59 = bf16[256,64,304]{0,2,1:T(8,128)(2,1)} copy(bf16[256,64,304]{2,1,0:T(8,128)(2,1)} %bitcast.85) | data formatting | bytes 19922944 | tf_op jit(solution)/shard_map/jit(_take)/gather | solution.py:91
  371.8 8.5 %broadcast_select_fusion = bf16[256,64,304]{0,2,1:T(8,128)(2,1)} fusion(bf16[256,64,304]{0,2,1:T(8,128)(2,1)} %copy.59, pred[256,64]{0,1:T(8,128)(4,1)S(1)} %compare_and_fusion), kind=kLoop, calls=%fused_computation.16 | loop fusion | flops 4980736 | bytes 19939328 | tf_op jit(solution)/shard_map/jit(_take)/select_n | solution.py:91
  380.4 9.3 %fusion.1 = f32[304,1,256]{2,0,1:T(8,128)S(1)} fusion(f32[256,304]{0,1:T(8,128)S(1)} %fusion.11, bf16[19456,304]{0,1:T(8,128)(2,1)} %param.26, bf16[256,19456]{0,1:T(8,128)(2,1)} %bitcast.87), kind=kOutput, calls=%fused_computation.19 | convolution fusion | flops 3028365312 | bytes 22413312 | tf_op jit(solution)/shard_map/dot_general | solution.py:93
  389.6 1.0 copy.62
  (58 shorter events, 1.5 us)
Async XLA Ops:
  0.6 182.1 %copy-start = (bf16[304,2432]{1,0:T(8,128)(2,1)S(1)}, bf16[304,2432]{1,0:T(8,128)(2,1)}, u32[]{:S(2)}) copy-start(bf16[304,2432]{1,0:T(8,128)(2,1)} %param.24) | copy-start | bytes 4435972
  0.6 43.8 %copy-start.3 = (s32[64,1,256]{2,1,0:T(1,128)S(1)}, s32[64,1,256]{2,1,0:T(1,128)}, u32[]{:S(2)}) copy-start(s32[64,1,256]{2,1,0:T(1,128)} %param.21) | copy-start | bytes 196612
  4.7 29.9 %all-to-all-start.1 = ((f32[1,128,2]{2,0,1:T(1,128)}), f32[1,128,2]{2,0,1:T(1,128)S(1)}, u32[]{:S(2)}, u32[]{:S(2)}) async-start(f32[1,128,2]{2,0,1:T(1,128)} %bitcast.11), calls=%async_computation.1 | async-start | bytes 131072 | tf_op jit(solution)/shard_map/all_to_all | solution.py:84
  18.0 45.6 %copy-start.5 = (f32[152]{0:T(256)S(1)}, f32[152]{0:T(256)}, u32[]{:S(2)}) copy-start(f32[152]{0:T(256)} %constant.98) | copy-start | bytes 1828
  18.0 45.6 %copy-start.6 = (f32[152]{0:T(256)S(1)}, f32[152]{0:T(256)}, u32[]{:S(2)}) copy-start(f32[152]{0:T(256)} %constant.99) | copy-start | bytes 1828
  18.1 45.6 %copy-start.7 = (f32[152]{0:T(256)S(1)}, f32[152]{0:T(256)}, u32[]{:S(2)}) copy-start(f32[152]{0:T(256)} %constant.100) | copy-start | bytes 1828
  34.6 28.7 %all-to-all-start = ((f32[5,256,128]{2,0,1:T(8,128)}), f32[5,256,128]{2,0,1:T(8,128)S(1)}, u32[]{:S(2)}, u32[]{:S(2)}) async-start(f32[5,256,128]{2,0,1:T(8,128)} %scatter_fusion), calls=%async_computation | async-start | bytes 2097152 | tf_op jit(solution)/shard_map/all_to_all | solution.py:83
  63.7 109.9 %copy-start.2 = (f32[304,304]{1,0:T(8,128)S(1)}, f32[304,304]{1,0:T(8,128)}, u32[]{:S(2)}) copy-start(f32[304,304]{1,0:T(8,128)} %param.23) | copy-start | bytes 1108996
  63.7 111.2 %copy-start.4 = (s32[64,1,256]{2,1,0:T(1,128)S(1)}, s32[64,1,256]{2,1,0:T(1,128)}, u32[]{:S(2)}) copy-start(s32[64,1,256]{2,1,0:T(1,128)} %param.22) | copy-start | bytes 196612
  174.2 6.9 %collective-permute-start.2 = (bf16[304,256]{1,0:T(8,128)(2,1)S(1)}, bf16[304,256]{1,0:T(8,128)(2,1)S(1)}, u32[]{:S(2)}, u32[]{:S(2)}) collective-permute-start(bf16[304,256]{1,0:T(8,128)(2,1)S(1)} %fusion.2), channel_id=1, source_target_pairs={{0,1},{1,0},{2,3},{3,2},{4,5},{5,4},{6,7},{7,6},{8,9},{9,8},{10,11... | collective-permute-start | bytes 466952 | tf_op jit(solution)/shard_map/ppermute | solution.py:39
  174.9 9.1 %collective-permute-start.1 = (bf16[304,256]{1,0:T(8,128)(2,1)S(1)}, bf16[304,256]{1,0:T(8,128)(2,1)S(1)}, u32[]{:S(2)}, u32[]{:S(2)}) collective-permute-start(bf16[304,256]{1,0:T(8,128)(2,1)S(1)} %fusion.2), channel_id=1, source_target_pairs={{8,0},{16,8},{24,16},{32,24},{40,32},{48,40},{56,48},{64,56},{72,6... | collective-permute-start | bytes 466952 | tf_op jit(solution)/shard_map/ppermute | solution.py:25
  178.5 5.5 %collective-permute-start = (bf16[304,256]{1,0:T(8,128)(2,1)S(1)}, bf16[304,256]{1,0:T(8,128)(2,1)S(1)}, u32[]{:S(2)}, u32[]{:S(2)}) collective-permute-start(bf16[304,256]{1,0:T(8,128)(2,1)S(1)} %fusion.2), channel_id=1, source_target_pairs={{0,8},{8,16},{16,24},{24,32},{32,40},{40,48},{48,56},{56,64},{64,7... | collective-permute-start | bytes 466952 | tf_op jit(solution)/shard_map/ppermute | solution.py:23
  181.1 84.5 %collective-permute-start.3 = (bf16[304,256]{1,0:T(8,128)(2,1)S(1)}, bf16[304,256]{1,0:T(8,128)(2,1)S(1)}, u32[]{:S(2)}, u32[]{:S(2)}) collective-permute-start(bf16[304,256]{1,0:T(8,128)(2,1)S(1)} %collective-permute-done.2), channel_id=1, source_target_pairs={{0,2},{2,0},{1,3},{3,1},{4,6},{6,4},{5,7},{7,5},{8,10},{10,8},{9,1... | collective-permute-start | bytes 466952 | tf_op jit(solution)/shard_map/ppermute | solution.py:39
  265.6 9.2 %collective-permute-start.4 = (bf16[304,256]{1,0:T(8,128)(2,1)S(1)}, bf16[304,256]{1,0:T(8,128)(2,1)S(1)}, u32[]{:S(2)}, u32[]{:S(2)}) collective-permute-start(bf16[304,256]{1,0:T(8,128)(2,1)S(1)} %collective-permute-done.3), channel_id=1, source_target_pairs={{0,4},{4,0},{1,5},{5,1},{2,6},{6,2},{3,7},{7,3},{8,12},{12,8},{9,1... | collective-permute-start | bytes 466952 | tf_op jit(solution)/shard_map/ppermute | solution.py:39
  274.9 15.2 %collective-permute-start.6 = (bf16[304,256]{1,0:T(8,128)(2,1)S(1)}, bf16[304,256]{1,0:T(8,128)(2,1)S(1)}, u32[]{:S(2)}, u32[]{:S(2)}) collective-permute-start(bf16[304,256]{1,0:T(8,128)(2,1)S(1)} %collective-permute-done.4), channel_id=1, source_target_pairs={{8,0},{16,8},{24,16},{32,24},{40,32},{48,40},{56,48},{64,56},{72,6... | collective-permute-start | bytes 466952 | tf_op jit(solution)/shard_map/ppermute | solution.py:25
  277.2 12.9 %collective-permute-start.5 = (bf16[304,256]{1,0:T(8,128)(2,1)S(1)}, bf16[304,256]{1,0:T(8,128)(2,1)S(1)}, u32[]{:S(2)}, u32[]{:S(2)}) collective-permute-start(bf16[304,256]{1,0:T(8,128)(2,1)S(1)} %collective-permute-done.4), channel_id=1, source_target_pairs={{0,8},{8,16},{16,24},{24,32},{32,40},{40,48},{48,56},{56,64},{64,7... | collective-permute-start | bytes 466952 | tf_op jit(solution)/shard_map/ppermute | solution.py:23
  380.4 10.3 %copy-start.1 = (bf16[304,2432]{1,0:T(8,128)(2,1)S(1)}, bf16[304,2432]{1,0:T(8,128)(2,1)}, u32[]{:S(2)}) copy-start(bf16[304,2432]{1,0:T(8,128)(2,1)} %param.24) | copy-start | bytes 4435972
where the time goes:
time: 393 us; the launch traced here: 391 us
  local copies, waits for them, and re-layouts  183 us (47%)
  other arithmetic  132 us (34%)
  starting transfers between devices  35.9 us (9%)
  matrix products  21.8 us (6%)
  waiting for transfers between devices  17.4 us (4%)
    gather x4, local copies, waits for them, and re-layouts, translate(): gathered = jnp.take(window_rows, picked, axis=0)  163 us
    reduce_sum x8, other arithmetic, block_check(): jnp.sum(cosine * charges[0][None] - sine_part * charges[1][None], axis=2)  101 us
    select_n x4, other arithmetic, translate(): gathered = jnp.take(window_rows, picked, axis=0)  18.8 us
    dot_general x2, matrix products, translate(): return jnp.dot(flat, operators, preferred_element_type=jnp.float32)  18.4 us
    all_to_all x1, waiting for transfers between devices, deliver(): lax.all_to_all(payload, ('box', 'depth'), split_axis=1, concat_axis=1, ti...  17.4 us
    scatter x1, local copies, waits for them, and re-layouts, local(): jnp.zeros((5, slots, row_count), jnp.float32).at[:, slot_index, :]  12.4 us
    all_to_all x1, starting transfers between devices, deliver(): lax.all_to_all(leaf_row, ('box', 'depth'), split_axis=1, concat_axis=1, t...  11.5 us
    all_to_all x1, starting transfers between devices, deliver(): lax.all_to_all(payload, ('box', 'depth'), split_axis=1, concat_axis=1, ti...  9.79 us
  transfers between devices with their start and end apart: 9, of which 1 were waited for; matrix products, arithmetic and copies ran while one was open for 31% of the time, Pallas kernels for 0%

commit v1 on v0

v1 whole, which is shorter than its diff:
```python
import functools

import jax
import jax.numpy as jnp
import numpy as np
from jax import lax
from jax.experimental import pallas as pl
from jax.experimental.pallas import tpu as pltpu
from jax.sharding import PartitionSpec as P
from numpy.polynomial import chebyshev, polynomial

GRID = 6
LANES = 384
VM = pl.BlockSpec(memory_space=pltpu.VMEM)
SM = pl.BlockSpec(memory_space=pltpu.SMEM)


def surface_index(grid_size):
    indices = np.arange(grid_size)
    lattice = np.stack(np.meshgrid(indices, indices, indices, indexing="ij"), -1).reshape(-1, 3)
    outside = np.any((lattice == 0) | (lattice == grid_size - 1), axis=1)
    return lattice[outside].astype(np.int32)


def node_coordinates(grid_size):
    middle = (grid_size - 1) / 2.0
    return ((np.arange(grid_size) - middle) * (1.5 / middle)).astype(np.float32)


def series(function, degree):
    fitted = chebyshev.Chebyshev.interpolate(function, degree, domain=[1.0, 12.0])
    return [float(value) for value in fitted.convert(kind=polynomial.Polynomial).coef]


HALF_SINE = series(lambda s: np.sin(np.sqrt(s) / 2) / (np.sqrt(s) / 2), 4)
HALF_COSINE = series(lambda s: np.cos(np.sqrt(s) / 2), 5)


def horner(coefficients, s):
    value = coefficients[-1] * s + coefficients[-2]
    for coefficient in coefficients[-3::-1]:
        value = value * s + coefficient
    return value


def waves(s):
    sine = horner(HALF_SINE, s)
    cosine = horner(HALF_COSINE, s)
    sine = sine * cosine
    cosine = cosine * cosine
    cosine = (cosine + cosine) - 1.0
    twice = cosine + cosine
    return (twice * cosine - 1.0) * lax.rsqrt(s), twice * sine


def pieces(value, count=3):
    terms = []
    for _ in range(count):
        terms.append(value.astype(jnp.bfloat16))
        value = value - terms[-1].astype(jnp.float32)
    return terms


def sources_kernel(capacity, table, positions, charges, counts, owner_row, owner_col, leaves, out, planes, depths, live_charges, values):
    nodes = node_coordinates(GRID)
    blocks, rows = positions.shape[1:]
    x, y, z = positions[0].T, positions[1].T, positions[2].T
    squares = []
    for node in nodes:
        delta = float(node) - y
        squares.append(delta * delta)
    for i, node in enumerate(nodes):
        delta = float(node) - x
        delta = delta * delta
        for j in range(len(nodes)):
            planes[i * len(nodes) + j] = delta + squares[j]
        delta = float(node) - z
        depths[i] = delta * delta
    live = lax.broadcasted_iota(jnp.int32, (rows, blocks), 0) < counts[...]
    for part in range(2):
        live_charges[part] = jnp.where(live, charges[part].T, 0.0)
    points = table.shape[1]
    values[...] = jnp.zeros_like(values)

    def one_point(p, carry):
        plane = table[0, p]
        depth = table[1, p]
        real = imaginary = None
        for chunk in range(rows // 8):
            place = pl.ds(8 * chunk, 8)
            cosine, sine = waves(planes[plane, place, :] + depths[depth, place, :])
            first = live_charges[0, place, :]
            second = live_charges[1, place, :]
            a = cosine * first - sine * second
            b = sine * first + cosine * second
            real = a if real is None else real + a
            imaginary = b if imaginary is None else imaginary + b
        values[pl.ds(p, 1), :] = jnp.sum(real, axis=0, keepdims=True)
        values[pl.ds(points + p, 1), :] = jnp.sum(imaginary, axis=0, keepdims=True)
        return carry

    lax.fori_loop(0, points, one_point, 0)
    values[pl.ds(2 * points, 1), :] = leaves[...].astype(jnp.float32)
    earlier = (owner_row[...] == owner_col[...]) & (
        lax.broadcasted_iota(jnp.int32, (blocks, blocks), 0)
        < lax.broadcasted_iota(jnp.int32, (blocks, blocks), 1)
    )
    rank = jnp.sum(jnp.where(earlier, 1.0, 0.0), axis=0, keepdims=True).astype(jnp.int32)
    slot = owner_row[...] * capacity + rank
    pick = jnp.where(lax.broadcasted_iota(jnp.int32, (out.shape[0], blocks), 0) == slot, 1.0, 0.0)
    pick = pick.astype(jnp.bfloat16)
    total = None
    for piece in pieces(values[...]):
        term = lax.dot_general(pick, piece, (((1,), (1,)), ((), ())), preferred_element_type=jnp.float32)
        total = term if total is None else total + term
    out[...] = total


def routed_sources(positions, charges, counts, owners, leaves, slots, capacity):
    index = surface_index(GRID)
    table = jnp.asarray(np.stack([index[:, 0] * GRID + index[:, 1], index[:, 2]]))
    blocks, rows = positions.shape[1:]
    return pl.pallas_call(
        functools.partial(sources_kernel, capacity),
        out_shape=jax.ShapeDtypeStruct((slots, LANES), jnp.float32),
        in_specs=[SM] + [VM] * 6,
        out_specs=VM,
        scratch_shapes=[
            pltpu.VMEM((GRID * GRID, rows, blocks), jnp.float32),
            pltpu.VMEM((GRID, rows, blocks), jnp.float32),
            pltpu.VMEM((2, rows, blocks), jnp.float32),
            pltpu.VMEM((LANES, blocks), jnp.float32),
        ],
        compiler_params=pltpu.CompilerParams(vmem_limit_bytes=32 << 20),
        name="sources",
    )(
        table,
        positions,
        charges,
        counts.reshape(1, blocks),
        owners.reshape(1, blocks),
        owners,
        leaves.reshape(1, blocks),
    )


def translate_kernel(batch, lists, windows, direct_ops, image_ops, out, gathered):
    step = pl.program_id(0)
    half = pl.num_programs(0) // 2
    channels = windows.shape[1]
    leaf_count = out.shape[1]
    window = windows[jnp.where(step >= half, 1, 0)]
    row = lax.broadcasted_iota(jnp.int32, (leaf_count, leaf_count), 0)
    for o in range(batch):
        chosen = lists[pl.ds(step * batch + o, 1), :]
        hot = jnp.concatenate(
            [
                jnp.where(row == chosen - part * leaf_count, 1.0, 0.0).astype(jnp.bfloat16)
                for part in range(3)
            ],
            axis=0,
        )
        picked = jnp.dot(window, hot, preferred_element_type=jnp.float32)
        gathered[pl.ds(o * channels, channels), :] = picked.astype(jnp.bfloat16)

    def apply(operators):
        term = jnp.dot(operators[...], gathered[...], preferred_element_type=jnp.float32)

        @pl.when(step == 0)
        def _():
            out[...] = term

        @pl.when(step > 0)
        def _():
            out[...] += term

    @pl.when(step < half)
    def _():
        apply(direct_ops)

    @pl.when(step >= half)
    def _():
        apply(image_ops)


def translate(lists, windows, direct_ops, image_ops):
    channels = windows.shape[1]
    offsets = lists.shape[0] // 2
    leaf_count = lists.shape[1]
    batch = 16
    count = offsets // batch
    return pl.pallas_call(
        functools.partial(translate_kernel, batch),
        out_shape=jax.ShapeDtypeStruct((channels, leaf_count), jnp.float32),
        grid=(2 * count,),
        in_specs=[
            pl.BlockSpec(lists.shape, lambda s: (0, 0)),
            pl.BlockSpec(windows.shape, lambda s: (0, 0, 0)),
            pl.BlockSpec((channels, batch * channels), lambda s: (0, jnp.minimum(s, count - 1))),
            pl.BlockSpec((channels, batch * channels), lambda s: (0, jnp.maximum(s - count, 0))),
        ],
        out_specs=pl.BlockSpec((channels, leaf_count), lambda s: (0, 0)),
        scratch_shapes=[pltpu.VMEM((batch * channels, leaf_count), jnp.bfloat16)],
        compiler_params=pltpu.CompilerParams(vmem_limit_bytes=48 << 20),
        name="translate",
    )(lists, windows, direct_ops, image_ops)


def local(
    positions,
    charges,
    counts,
    owners,
    leaves,
    near_lists,
    image_lists,
    upward,
    child_ops,
    direct_ops,
    image_ops,
):
    box_count = lax.axis_size("box")
    depth_count = lax.axis_size("depth")
    devices = box_count * depth_count
    blocks = positions.shape[1]
    capacity = 2 * blocks // devices
    slots = devices * capacity
    leaf_count = near_lists.shape[2]
    channels = upward.shape[0]
    sent = routed_sources(positions, charges, counts, owners, leaves, slots, capacity)
    arrived = lax.all_to_all(
        sent.reshape(devices, capacity * LANES),
        ("box", "depth"),
        split_axis=0,
        concat_axis=0,
        tiled=True,
    ).reshape(slots, LANES)
    members = (
        arrived[:, channels : channels + 1]
        == jnp.arange(leaf_count, dtype=jnp.float32)[None, :]
    ).astype(jnp.float32)
    raised = lax.dot_general(
        upward, arrived[:, :channels], (((1,), (1,)), ((), ())), precision=lax.Precision.HIGHEST
    )
    multipole = jnp.dot(raised, members, precision=lax.Precision.HIGHEST).astype(jnp.bfloat16)
    children = (
        multipole.reshape(channels, leaf_count // 8, 8)
        .transpose(0, 2, 1)
        .reshape(channels * 8, leaf_count // 8)
    )
    parents = jnp.dot(child_ops, children, preferred_element_type=jnp.float32)

    def routed(shift, mirror):
        pairs = []
        for box in range(box_count):
            for depth in range(depth_count):
                if 0 <= box + shift < box_count:
                    other = depth_count - 1 - depth if mirror else depth
                    pairs.append((box * depth_count + depth, (box + shift) * depth_count + other))
        return lax.ppermute(multipole, ("box", "depth"), pairs)

    windows = jnp.stack(
        [
            jnp.concatenate([routed(1, False), multipole, routed(-1, False)], axis=1),
            jnp.concatenate([routed(1, True), routed(0, True), routed(-1, True)], axis=1),
        ]
    )
    lists = jnp.concatenate([near_lists[:, 0, :], image_lists[:, 0, :]], axis=0)
    potentials = translate(lists, windows, direct_ops.T, image_ops.T)
    return (potentials[:, None, :], parents[:, None, :])


def solution(mesh):
    return jax.shard_map(
        local,
        mesh=mesh,
        in_specs=(
            P(None, ("box", "depth"), None),
            P(None, ("box", "depth"), None),
            P(("box", "depth")),
            P(("box", "depth"), None),
            P(("box", "depth")),
            P(None, "depth", "box"),
            P(None, "depth", "box"),
            P(),
            P(),
            P(),
            P(),
        ),
        out_specs=(P(None, "depth", "box"), P(None, "depth", "box")),
        check_vma=False,
    )
```

time: 393 us -> 102 us (0.26)
  local copies, waits for them, and re-layouts: 183 us -> 8.42 us
  other arithmetic: 132 us -> 1.1 us
  Pallas kernels: 0 us -> 43.6 us
  matrix products: 21.8 us -> 2.22 us
  starting transfers between devices: 35.9 us -> 27.1 us
    gather x4 -> x0, local copies, waits for them, and re-layouts: 163 us -> none  [translate(): gathered = jnp.take(window_rows, picked, axis=0)]
    reduce_sum x9 -> x0, other arithmetic: 102 us -> none  [the longest x8 101 us: block_check(): jnp.sum(cosine * charges[0][None] - sine_part * charges[1][None], axis=2)]
    pallas_call x0 -> x2, Pallas kernels: none -> 43.6 us  [the longest x1 27.5 us: translate(): pl.pallas_call(functools.partial(translate_kernel, batch), out_shape=jax....]
    dot_general x4 -> x2, matrix products: 20.6 us -> 1.04 us  [the longest x1 0.67 us: local(): lax.dot_general(upward, arrived[:, :channels], (((1,), (1,)), ((), ())),...]
    select_n x5 -> x0, other arithmetic: 19.4 us -> none  [the longest x4 18.8 us: translate(): gathered = jnp.take(window_rows, picked, axis=0)]
    scatter x2 -> x0, local copies, waits for them, and re-layouts: 13.3 us -> none  [the longest x1 12.4 us: local(): jnp.zeros((5, slots, row_count), jnp.float32).at[:, slot_index, :]]
    all_to_all x2 -> x1, starting transfers between devices: 21.3 us -> 11.5 us  [local(): lax.all_to_all(sent.reshape(devices, capacity * LANES), ('box', 'depth'),...]
    ppermute x7 -> x5, waiting for transfers between devices: 0.02 us -> 5.72 us  [routed(): return lax.ppermute(multipole, ('box', 'depth'), pairs)]
  transfers between devices with their start and end apart: 9 -> 6, of which waited for: 1 -> 3; matrix products, arithmetic and copies ran while one was open for 31% -> 2% of each run, Pallas kernels for 0% -> 0%
where the time goes in v1:
time: 102 us; the launch traced here: 101 us
  Pallas kernels  43.6 us (43%)
  starting transfers between devices  27.1 us (27%)
  waiting for transfers between devices  18.2 us (18%)
  local copies, waits for them, and re-layouts  8.42 us (8%)
  matrix products  2.22 us (2%)
  other arithmetic  1.1 us (1%)
    pallas_call x1, Pallas kernels, translate(): pl.pallas_call(functools.partial(translate_kernel, batch), out_shape=jax....  27.5 us
    pallas_call x1, Pallas kernels, routed_sources(): pl.pallas_call(functools.partial(sources_kernel, capacity), out_shape=jax...  16.1 us
    ppermute x5, starting transfers between devices, routed(): return lax.ppermute(multipole, ('box', 'depth'), pairs)  15.6 us
    all_to_all x1, waiting for transfers between devices, local(): lax.all_to_all(sent.reshape(devices, capacity * LANES), ('box', 'depth'),...  12.4 us
    all_to_all x1, starting transfers between devices, local(): lax.all_to_all(sent.reshape(devices, capacity * LANES), ('box', 'depth'),...  11.5 us
    unnamed x23, local copies, waits for them, and re-layouts  6.44 us
    ppermute x5, waiting for transfers between devices, routed(): return lax.ppermute(multipole, ('box', 'depth'), pairs)  5.72 us
  transfers between devices with their start and end apart: 6, of which 3 were waited for; matrix products, arithmetic and copies ran while one was open for 2% of the time, Pallas kernels for 0%

profile of v1, /device:TPU:1, one launch (start us, length us, event | category | flops | bytes accessed | tf_op | source)
XLA Modules:
  0.0 101.4 jit_solution(11851352085506223374)
XLA Ops:
  0.6 0.0 copy-start
  0.6 0.0 copy-start.8
  0.7 0.9 copy.24.owner_col
  1.5 0.0 copy-start.1
  1.6 0.9 copy-done.1
  2.5 0.0 copy-start.2
  2.5 0.9 copy-done.2
  3.4 0.0 copy-start.3
  3.4 0.7 copy-done.3
  4.1 0.0 copy-start.4
  4.1 0.7 copy-done.4
  4.7 0.0 copy-start.5
  4.7 0.7 copy-done.5
  5.4 0.0 copy-start.6
  5.4 0.7 copy-done.6
  6.0 0.0 copy-start.9
  6.0 16.1 %sources.1 = f32[256,384]{1,0:T(8,128)S(1)} custom-call(s32[2,152]{1,0:T(2,128)S(1)} %copy-done.3, f32[3,128,128]{2,1,0:T(8,128)S(1)} %copy-done.1, f32[2,128,128]{2,1,0:T(8,128)S(1)} %copy-done.2, s32[1,128]{1,0:T(1,128)S(1)} %bitcast.29, s32[1,128]{1,0:T(1,128)S(1)} %bitcast.28, s32[128,1]{1,0:T(8,128)S(1)} %copy.24.owner_col, s32[1,128]{1,0:T(1,128)S(1)} %bitcast.30), custom_call_target="tpu_custom_call" | custom-call | tf_op jit(solution)/shard_map/sources/pallas_call | solution.py:123
  22.1 1.1 %all_to_all.8 = f32[128,1,768]{2,1,0:T(1,128)} reshape(f32[256,384]{1,0:T(8,128)S(1)} %sources.1) | data formatting | bytes 786432 | tf_op jit(solution)/shard_map/all_to_all | solution.py:231
  23.2 0.0 copy-start.7
  23.2 11.5 %all-to-all-start = ((f32[128,1,768]{2,1,0:T(1,128)}), f32[128,1,768]{2,1,0:T(1,128)S(1)}, u32[]{:S(2)}, u32[]{:S(2)}) async-start(f32[128,1,768]{2,1,0:T(1,128)} %all_to_all.8), calls=%async_computation | async-start | bytes 786432 | tf_op jit(solution)/shard_map/all_to_all | solution.py:231
  34.7 0.0 copy-done.8
  34.7 0.0 copy-done.9
  34.8 12.4 %all-to-all-done = f32[128,1,768]{2,1,0:T(1,128)S(1)} async-done(((f32[128,1,768]{2,1,0:T(1,128)}), f32[128,1,768]{2,1,0:T(1,128)S(1)}, u32[]{:S(2)}, u32[]{:S(2)}) %all-to-all-start) | async-done | bytes 393248 | tf_op jit(solution)/shard_map/all_to_all | solution.py:231
  47.2 0.9 reduce
  48.2 0.1 reshape.30
  48.2 0.2 slice_reduce_fusion
  48.4 0.0 copy-done.7
  48.4 0.7 fusion.1
  49.1 0.4 convolution_convert_fusion
  49.5 2.1 %collective-permute-start = (bf16[304,256]{1,0:T(8,128)(2,1)S(1)}, bf16[304,256]{1,0:T(8,128)(2,1)S(1)}, u32[]{:S(2)}, u32[]{:S(2)}) collective-permute-start(bf16[304,256]{1,0:T(8,128)(2,1)S(1)} %convolution_convert_fusion), channel_id=1, source_target_pairs={{0,8},{1,9},{2,10},{3,11},{4,12},{5,13},{6,14},{7,15},{8,16},{9,17... | collective-permute-start | bytes 466952 | tf_op jit(solution)/shard_map/ppermute | solution.py:260
  51.6 2.2 %collective-permute-start.1 = (bf16[304,256]{1,0:T(8,128)(2,1)S(1)}, bf16[304,256]{1,0:T(8,128)(2,1)S(1)}, u32[]{:S(2)}, u32[]{:S(2)}) collective-permute-start(bf16[304,256]{1,0:T(8,128)(2,1)S(1)} %convolution_convert_fusion), channel_id=1, source_target_pairs={{8,0},{9,1},{10,2},{11,3},{12,4},{13,5},{14,6},{15,7},{16,8},{17,9... | collective-permute-start | bytes 466952 | tf_op jit(solution)/shard_map/ppermute | solution.py:260
  53.8 4.2 %collective-permute-start.2 = (bf16[304,256]{1,0:T(8,128)(2,1)S(1)}, bf16[304,256]{1,0:T(8,128)(2,1)S(1)}, u32[]{:S(2)}, u32[]{:S(2)}) collective-permute-start(bf16[304,256]{1,0:T(8,128)(2,1)S(1)} %convolution_convert_fusion), channel_id=1, source_target_pairs={{0,15},{1,14},{2,13},{3,12},{4,11},{5,10},{6,9},{7,8},{8,23},{9,22... | collective-permute-start | bytes 466952 | tf_op jit(solution)/shard_map/ppermute | solution.py:260
  58.0 3.1 %collective-permute-start.3 = (bf16[304,256]{1,0:T(8,128)(2,1)S(1)}, bf16[304,256]{1,0:T(8,128)(2,1)S(1)}, u32[]{:S(2)}, u32[]{:S(2)}) collective-permute-start(bf16[304,256]{1,0:T(8,128)(2,1)S(1)} %convolution_convert_fusion), channel_id=1, source_target_pairs={{0,7},{1,6},{2,5},{3,4},{4,3},{5,2},{6,1},{7,0},{8,15},{9,14},{10,... | collective-permute-start | bytes 466952 | tf_op jit(solution)/shard_map/ppermute | solution.py:260
  61.2 3.9 %collective-permute-start.4 = (bf16[304,256]{1,0:T(8,128)(2,1)S(1)}, bf16[304,256]{1,0:T(8,128)(2,1)S(1)}, u32[]{:S(2)}, u32[]{:S(2)}) collective-permute-start(bf16[304,256]{1,0:T(8,128)(2,1)S(1)} %convolution_convert_fusion), channel_id=1, source_target_pairs={{8,7},{9,6},{10,5},{11,4},{12,3},{13,2},{14,1},{15,0},{16,15},{17,... | collective-permute-start | bytes 466952 | tf_op jit(solution)/shard_map/ppermute | solution.py:260
  65.1 0.2 copy.26
  65.3 0.5 copy.27
  65.7 0.0 copy-done
  65.7 1.2 %convolution_bitcast_fusion = f32[304,1,32]{0,2,1:T(8,128)} fusion(bf16[304,2432]{1,0:T(8,128)(2,1)S(1)} %copy-done, bf16[304,8,32]{2,1,0:T(8,128)(2,1)S(1)} %copy.27), kind=kOutput, calls=%fused_computation.1 | convolution fusion | flops 47316992 | bytes 1673216 | tf_op jit(solution)/shard_map/dot_general | solution.py:251
  66.9 0.0 collective-permute-done
  66.9 0.0 collective-permute-done.1
  67.0 0.0 collective-permute-done.2
  67.0 0.5 collective-permute-done.3
  67.5 5.2 %collective-permute-done.4 = bf16[304,256]{1,0:T(8,128)(2,1)S(1)} collective-permute-done((bf16[304,256]{1,0:T(8,128)(2,1)S(1)}, bf16[304,256]{1,0:T(8,128)(2,1)S(1)}, u32[]{:S(2)}, u32[]{:S(2)}) %collective-permute-start.4) | collective-permute-done | bytes 155680 | tf_op jit(solution)/shard_map/ppermute | solution.py:260
  72.7 0.1 pad_maximum_fusion.windows
  72.8 27.5 %translate.1 = f32[304,256]{1,0:T(8,128)S(1)} custom-call(s32[128,256]{1,0:T(8,128)S(1)} %pad_add_fusion.lists, bf16[2,304,768]{2,1,0:T(8,128)(2,1)S(1)} %pad_maximum_fusion.windows, bf16[304,19456]{1,0:T(8,128)(2,1)} %bitcast.31, bf16[304,19456]{1,0:T(8,128)(2,1)} %bitcast.32), custom_call_target="tpu_custom_call" | custom-call | tf_op jit(solution)/shard_map/translate/pallas_call | solution.py:192
  100.4 1.0 %copy.28 = f32[304,1,256]{2,1,0:T(1,128)} copy(f32[304,1,256]{2,0,1:T(8,128)S(1)} %bitcast.27) | data formatting | bytes 622592
  (4 shorter events, 0.1 us)
Async XLA Ops:
  0.6 65.1 %copy-start = (bf16[304,2432]{1,0:T(8,128)(2,1)S(1)}, bf16[304,2432]{1,0:T(8,128)(2,1)}, u32[]{:S(2)}) copy-start(bf16[304,2432]{1,0:T(8,128)(2,1)} %param.20) | copy-start | bytes 4435972
  0.6 34.1 %copy-start.8 = (s32[64,1,256]{2,1,0:T(1,128)S(1)}, s32[64,1,256]{2,1,0:T(1,128)}, u32[]{:S(2)}) copy-start(s32[64,1,256]{2,1,0:T(1,128)} %param.18) | copy-start | bytes 196612
  1.5 0.9 copy-start.1
  2.5 0.9 copy-start.2
  3.4 0.7 copy-start.3
  4.1 0.7 copy-start.4
  4.7 0.7 copy-start.5
  5.4 0.7 copy-start.6
  6.0 28.7 %copy-start.9 = (s32[64,1,256]{2,1,0:T(1,128)S(1)}, s32[64,1,256]{2,1,0:T(1,128)}, u32[]{:S(2)}) copy-start(s32[64,1,256]{2,1,0:T(1,128)} %param.17) | copy-start | bytes 196612
  23.2 25.2 %copy-start.7 = (f32[304,304]{1,0:T(8,128)S(1)}, f32[304,304]{1,0:T(8,128)}, u32[]{:S(2)}) copy-start(f32[304,304]{1,0:T(8,128)} %param.19) | copy-start | bytes 1108996
  23.2 24.0 %all-to-all-start = ((f32[128,1,768]{2,1,0:T(1,128)}), f32[128,1,768]{2,1,0:T(1,128)S(1)}, u32[]{:S(2)}, u32[]{:S(2)}) async-start(f32[128,1,768]{2,1,0:T(1,128)} %all_to_all.8), calls=%async_computation | async-start | bytes 786432 | tf_op jit(solution)/shard_map/all_to_all | solution.py:231
  49.5 17.5 %collective-permute-start = (bf16[304,256]{1,0:T(8,128)(2,1)S(1)}, bf16[304,256]{1,0:T(8,128)(2,1)S(1)}, u32[]{:S(2)}, u32[]{:S(2)}) collective-permute-start(bf16[304,256]{1,0:T(8,128)(2,1)S(1)} %convolution_convert_fusion), channel_id=1, source_target_pairs={{0,8},{1,9},{2,10},{3,11},{4,12},{5,13},{6,14},{7,15},{8,16},{9,17... | collective-permute-start | bytes 466952 | tf_op jit(solution)/shard_map/ppermute | solution.py:260
  51.6 15.3 %collective-permute-start.1 = (bf16[304,256]{1,0:T(8,128)(2,1)S(1)}, bf16[304,256]{1,0:T(8,128)(2,1)S(1)}, u32[]{:S(2)}, u32[]{:S(2)}) collective-permute-start(bf16[304,256]{1,0:T(8,128)(2,1)S(1)} %convolution_convert_fusion), channel_id=1, source_target_pairs={{8,0},{9,1},{10,2},{11,3},{12,4},{13,5},{14,6},{15,7},{16,8},{17,9... | collective-permute-start | bytes 466952 | tf_op jit(solution)/shard_map/ppermute | solution.py:260
  53.8 13.1 %collective-permute-start.2 = (bf16[304,256]{1,0:T(8,128)(2,1)S(1)}, bf16[304,256]{1,0:T(8,128)(2,1)S(1)}, u32[]{:S(2)}, u32[]{:S(2)}) collective-permute-start(bf16[304,256]{1,0:T(8,128)(2,1)S(1)} %convolution_convert_fusion), channel_id=1, source_target_pairs={{0,15},{1,14},{2,13},{3,12},{4,11},{5,10},{6,9},{7,8},{8,23},{9,22... | collective-permute-start | bytes 466952 | tf_op jit(solution)/shard_map/ppermute | solution.py:260
  58.0 9.4 %collective-permute-start.3 = (bf16[304,256]{1,0:T(8,128)(2,1)S(1)}, bf16[304,256]{1,0:T(8,128)(2,1)S(1)}, u32[]{:S(2)}, u32[]{:S(2)}) collective-permute-start(bf16[304,256]{1,0:T(8,128)(2,1)S(1)} %convolution_convert_fusion), channel_id=1, source_target_pairs={{0,7},{1,6},{2,5},{3,4},{4,3},{5,2},{6,1},{7,0},{8,15},{9,14},{10,... | collective-permute-start | bytes 466952 | tf_op jit(solution)/shard_map/ppermute | solution.py:260
  61.2 11.5 %collective-permute-start.4 = (bf16[304,256]{1,0:T(8,128)(2,1)S(1)}, bf16[304,256]{1,0:T(8,128)(2,1)S(1)}, u32[]{:S(2)}, u32[]{:S(2)}) collective-permute-start(bf16[304,256]{1,0:T(8,128)(2,1)S(1)} %convolution_convert_fusion), channel_id=1, source_target_pairs={{8,7},{9,6},{10,5},{11,4},{12,3},{13,2},{14,1},{15,0},{16,15},{17,... | collective-permute-start | bytes 466952 | tf_op jit(solution)/shard_map/ppermute | solution.py:260

commit v2 on v1

--- a/solution.py
+++ b/solution.py
@@ -106,23 +106,23 @@
         < lax.broadcasted_iota(jnp.int32, (blocks, blocks), 1)
     )
     rank = jnp.sum(jnp.where(earlier, 1.0, 0.0), axis=0, keepdims=True).astype(jnp.int32)
-    slot = owner_row[...] * capacity + rank
-    pick = jnp.where(lax.broadcasted_iota(jnp.int32, (out.shape[0], blocks), 0) == slot, 1.0, 0.0)
-    pick = pick.astype(jnp.bfloat16)
-    total = None
-    for piece in pieces(values[...]):
-        term = lax.dot_general(pick, piece, (((1,), (1,)), ((), ())), preferred_element_type=jnp.float32)
-        total = term if total is None else total + term
-    out[...] = total
-
-
-def routed_sources(positions, charges, counts, owners, leaves, slots, capacity):
+    terms = pieces(values[...])
+    device = lax.broadcasted_iota(jnp.int32, (out.shape[0], blocks), 0)
+    for place in range(capacity):
+        pick = jnp.where((device == owner_row[...]) & (rank == place), 1.0, 0.0).astype(jnp.bfloat16)
+        out[:, place, :] = sum(
+            lax.dot_general(pick, term, (((1,), (1,)), ((), ())), preferred_element_type=jnp.float32)
+            for term in terms
+        )
+
+
+def routed_sources(positions, charges, counts, owners, leaves, devices, capacity):
     index = surface_index(GRID)
     table = jnp.asarray(np.stack([index[:, 0] * GRID + index[:, 1], index[:, 2]]))
     blocks, rows = positions.shape[1:]
     return pl.pallas_call(
         functools.partial(sources_kernel, capacity),
-        out_shape=jax.ShapeDtypeStruct((slots, LANES), jnp.float32),
+        out_shape=jax.ShapeDtypeStruct((devices, capacity, LANES), jnp.float32),
         in_specs=[SM] + [VM] * 6,
         out_specs=VM,
         scratch_shapes=[
@@ -144,12 +144,153 @@
     )
 
 
+def exchange_kernel(
+    sent, upward, windows, multipole, arrived, send_sem, arrive_sem, halo_send, halo_recv
+):
+    box, depth = lax.axis_index("box"), lax.axis_index("depth")
+    boxes, depths = lax.axis_size("box"), lax.axis_size("depth")
+    devices, capacity, _ = sent.shape
+    channels, leaf_count = multipole.shape
+    me = box * depths + depth
+
+    def route(j, carry):
+        target = lax.rem(me + j, devices)
+        pltpu.make_async_remote_copy(
+            src_ref=sent.at[target],
+            dst_ref=arrived.at[me],
+            send_sem=send_sem,
+            recv_sem=arrive_sem,
+            device_id=(target // depths, lax.rem(target, depths)),
+            device_id_type=pl.DeviceIdType.MESH,
+        ).start()
+        return carry
+
+    lax.fori_loop(1, devices, route, 0)
+    arrived[me] = sent[me]
+    others = pl.ds(0, devices - 1)
+    every = pltpu.make_async_remote_copy(
+        src_ref=sent.at[others],
+        dst_ref=arrived.at[others],
+        send_sem=send_sem,
+        recv_sem=arrive_sem,
+        device_id=(lax.rem(box + 1, boxes), depth),
+        device_id_type=pl.DeviceIdType.MESH,
+    )
+    every.wait_send()
+    every.wait_recv()
+    values = jnp.concatenate([arrived[:, place, :] for place in range(capacity)], axis=0)
+    leaf = values[:, channels : channels + 1].astype(jnp.int32)
+    members = jnp.where(
+        lax.broadcasted_iota(jnp.int32, (devices * capacity, leaf_count), 1) == leaf, 1.0, 0.0
+    ).astype(jnp.bfloat16)
+    raised = lax.dot_general(
+        upward[...],
+        values[:, :channels],
+        (((1,), (1,)), ((), ())),
+        precision=lax.Precision.HIGHEST,
+        preferred_element_type=jnp.float32,
+    )
+    summed = sum(
+        jnp.dot(term, members, preferred_element_type=jnp.float32) for term in pieces(raised)
+    )
+    own = summed.astype(jnp.bfloat16)
+    multipole[...] = own
+    windows[0, 1] = own
+
+    def copy(number, source, place, device):
+        return pltpu.make_async_remote_copy(
+            src_ref=source,
+            dst_ref=windows.at[place],
+            send_sem=halo_send.at[number],
+            recv_sem=halo_recv.at[number],
+            device_id=device,
+            device_id_type=pl.DeviceIdType.MESH,
+        )
+
+    def beside(number, source, slab, device_depth):
+        to_right = copy(number, source, (slab, 0), (box + 1, device_depth))
+        to_left = copy(number + 1, source, (slab, 2), (box - 1, device_depth))
+        return to_right, to_left
+
+    mirror = copy(4, multipole, (1, 1), (box, depths - 1 - depth))
+    direct = beside(0, multipole, 0, depth)
+    image = beside(2, windows.at[1, 1], 1, depth)
+    has_left, has_right = box > 0, box < boxes - 1
+    blank = jnp.zeros((channels, leaf_count), jnp.bfloat16)
+
+    mirror.start()
+
+    @pl.when(has_right)
+    def _():
+        direct[0].start()
+
+    @pl.when(has_left)
+    def _():
+        direct[1].start()
+
+    @pl.when(jnp.logical_not(has_left))
+    def _():
+        windows[0, 0] = blank
+        windows[1, 0] = blank
+
+    @pl.when(jnp.logical_not(has_right))
+    def _():
+        windows[0, 2] = blank
+        windows[1, 2] = blank
+
+    mirror.wait_recv()
+
+    @pl.when(has_right)
+    def _():
+        image[0].start()
+
+    @pl.when(has_left)
+    def _():
+        image[1].start()
+
+    for pair in (direct, image):
+
+        @pl.when(has_left)
+        def _():
+            pair[0].wait_recv()
+            pair[1].wait_send()
+
+        @pl.when(has_right)
+        def _():
+            pair[1].wait_recv()
+            pair[0].wait_send()
+
+    mirror.wait_send()
+
+
+def exchange(sent, upward, leaf_count):
+    channels = upward.shape[0]
+    return pl.pallas_call(
+        exchange_kernel,
+        out_shape=(
+            jax.ShapeDtypeStruct((2, 3, channels, leaf_count), jnp.bfloat16),
+            jax.ShapeDtypeStruct((channels, leaf_count), jnp.bfloat16),
+        ),
+        in_specs=[VM, VM],
+        out_specs=(VM, VM),
+        scratch_shapes=[
+            pltpu.VMEM(sent.shape, jnp.float32),
+            pltpu.SemaphoreType.DMA,
+            pltpu.SemaphoreType.DMA,
+            pltpu.SemaphoreType.DMA((5,)),
+            pltpu.SemaphoreType.DMA((5,)),
+        ],
+        compiler_params=pltpu.CompilerParams(vmem_limit_bytes=32 << 20, has_side_effects=True),
+        name="exchange",
+    )(sent, upward)
+
+
 def translate_kernel(batch, lists, windows, direct_ops, image_ops, out, gathered):
     step = pl.program_id(0)
     half = pl.num_programs(0) // 2
-    channels = windows.shape[1]
-    leaf_count = out.shape[1]
-    window = windows[jnp.where(step >= half, 1, 0)]
+    channels, leaf_count = out.shape
+    slab = jnp.where(step >= half, 1, 0)
+    window = jnp.concatenate([windows[slab, part] for part in range(3)], axis=1)
     row = lax.broadcasted_iota(jnp.int32, (leaf_count, leaf_count), 0)
     for o in range(batch):
         chosen = lists[pl.ds(step * batch + o, 1), :]
@@ -184,9 +325,8 @@
 
 
 def translate(lists, windows, direct_ops, image_ops):
-    channels = windows.shape[1]
+    channels, leaf_count = windows.shape[2:]
     offsets = lists.shape[0] // 2
-    leaf_count = lists.shape[1]
     batch = 16
     count = offsets // batch
     return pl.pallas_call(
@@ -195,7 +335,7 @@
         grid=(2 * count,),
         in_specs=[
             pl.BlockSpec(lists.shape, lambda s: (0, 0)),
-            pl.BlockSpec(windows.shape, lambda s: (0, 0, 0)),
+            pl.BlockSpec(windows.shape, lambda s: (0, 0, 0, 0)),
             pl.BlockSpec((channels, batch * channels), lambda s: (0, jnp.minimum(s, count - 1))),
             pl.BlockSpec((channels, batch * channels), lambda s: (0, jnp.maximum(s - count, 0))),
         ],
@@ -224,25 +364,10 @@
     devices = box_count * depth_count
     blocks = positions.shape[1]
     capacity = 2 * blocks // devices
-    slots = devices * capacity
     leaf_count = near_lists.shape[2]
     channels = upward.shape[0]
-    sent = routed_sources(positions, charges, counts, owners, leaves, slots, capacity)
-    arrived = lax.all_to_all(
-        sent.reshape(devices, capacity * LANES),
-        ("box", "depth"),
-        split_axis=0,
-        concat_axis=0,
-        tiled=True,
-    ).reshape(slots, LANES)
-    members = (
-        arrived[:, channels : channels + 1]
-        == jnp.arange(leaf_count, dtype=jnp.float32)[None, :]
-    ).astype(jnp.float32)
-    raised = lax.dot_general(
-        upward, arrived[:, :channels], (((1,), (1,)), ((), ())), precision=lax.Precision.HIGHEST
-    )
-    multipole = jnp.dot(raised, members, precision=lax.Precision.HIGHEST).astype(jnp.bfloat16)
+    sent = routed_sources(positions, charges, counts, owners, leaves, devices, capacity)
+    windows, multipole = exchange(sent, upward, leaf_count)
     children = (
         multipole.reshape(channels, leaf_count // 8, 8)
         .transpose(0, 2, 1)
@@ -250,21 +375,6 @@
     )
     parents = jnp.dot(child_ops, children, preferred_element_type=jnp.float32)
 
-    def routed(shift, mirror):
-        pairs = []
-        for box in range(box_count):
-            for depth in range(depth_count):
-                if 0 <= box + shift < box_count:
-                    other = depth_count - 1 - depth if mirror else depth
-                    pairs.append((box * depth_count + depth, (box + shift) * depth_count + other))
-        return lax.ppermute(multipole, ("box", "depth"), pairs)
-
-    windows = jnp.stack(
-        [
-            jnp.concatenate([routed(1, False), multipole, routed(-1, False)], axis=1),
-            jnp.concatenate([routed(1, True), routed(0, True), routed(-1, True)], axis=1),
-        ]
-    )
     lists = jnp.concatenate([near_lists[:, 0, :], image_lists[:, 0, :]], axis=0)
     potentials = translate(lists, windows, direct_ops.T, image_ops.T)
     return (potentials[:, None, :], parents[:, None, :])

time: 102 us -> 89.6 us (0.88)
  Pallas kernels: 43.6 us -> 79.6 us
  starting transfers between devices: 27.1 us -> 0 us
  waiting for transfers between devices: 18.2 us -> 0 us
  other arithmetic: 1.1 us -> 0.01 us
  matrix products: 2.22 us -> 1.17 us
    pallas_call x0 -> x1, Pallas kernels: none -> 35.9 us  [exchange(): pl.pallas_call(exchange_kernel, out_shape=(jax.ShapeDtypeStruct((2, 3, ch...]
    ppermute x5 -> x0, starting transfers between devices: 15.6 us -> none  [routed(): return lax.ppermute(multipole, ('box', 'depth'), pairs)]
    all_to_all x1 -> x0, waiting for transfers between devices: 12.4 us -> none  [local(): lax.all_to_all(sent.reshape(devices, capacity * LANES), ('box', 'depth'),...]
    all_to_all x1 -> x0, starting transfers between devices: 11.5 us -> none  [local(): lax.all_to_all(sent.reshape(devices, capacity * LANES), ('box', 'depth'),...]
    ppermute x5 -> x0, waiting for transfers between devices: 5.72 us -> none  [routed(): return lax.ppermute(multipole, ('box', 'depth'), pairs)]
    all_to_all x1 -> x0, local copies, waits for them, and re-layouts: 1.13 us -> none  [local(): lax.all_to_all(sent.reshape(devices, capacity * LANES), ('box', 'depth'),...]
    dot_general x2 -> x0, matrix products: 1.04 us -> none  [the longest x1 0.67 us: local(): lax.dot_general(upward, arrived[:, :channels], (((1,), (1,)), ((), ())),...]
    unnamed x23 -> x19, local copies, waits for them, and re-layouts: 6.44 us -> 7.31 us
  transfers between devices with their start and end apart: 6 -> 0, of which waited for: 3 -> 0; matrix products, arithmetic and copies ran while one was open for 2% -> 0% of each run, Pallas kernels for 0% -> 0%
where the time goes in v2:
time: 89.6 us; the launch traced here: 89.4 us
  Pallas kernels  79.6 us (89%)
  local copies, waits for them, and re-layouts  7.92 us (9%)
  matrix products  1.17 us (1%)
    pallas_call x1, Pallas kernels, exchange(): pl.pallas_call(exchange_kernel, out_shape=(jax.ShapeDtypeStruct((2, 3, ch...  35.9 us
    pallas_call x1, Pallas kernels, translate(): pl.pallas_call(functools.partial(translate_kernel, batch), out_shape=jax....  27.5 us
    pallas_call x1, Pallas kernels, routed_sources(): pl.pallas_call(functools.partial(sources_kernel, capacity), out_shape=jax...  16.1 us
    unnamed x19, local copies, waits for them, and re-layouts  7.31 us

profile of v2, /device:TPU:1, one launch (start us, length us, event | category | flops | bytes accessed | tf_op | source)
XLA Modules:
  0.0 89.4 jit_solution(8581526000563868468)
XLA Ops:
  0.6 0.0 copy-start
  0.6 0.0 copy-start.1
  0.7 0.9 %copy.16.owner_col = s32[128,1]{1,0:T(8,128)S(1)} copy(s32[128,1]{0,1:T(1,128)} %param.15) | data formatting | bytes 1024 | tf_op args[3]
  1.6 0.9 copy_bitcast_fusion
  2.5 0.0 copy-start.2
  2.5 0.9 %copy-done.2 = f32[3,128,128]{2,1,0:T(8,128)S(1)} copy-done((f32[3,128,128]{2,1,0:T(8,128)S(1)}, f32[3,128,128]{2,1,0:T(8,128)}, u32[]{:S(2)}) %copy-start.2) | copy-done | bytes 196632
  3.4 0.0 copy-start.3
  3.4 0.9 %copy-done.3 = f32[2,128,128]{2,1,0:T(8,128)S(1)} copy-done((f32[2,128,128]{2,1,0:T(8,128)S(1)}, f32[2,128,128]{2,1,0:T(8,128)}, u32[]{:S(2)}) %copy-start.3) | copy-done | bytes 131096
  4.3 0.0 copy-start.4
  4.3 0.7 copy-done.4
  5.0 0.0 copy-start.5
  5.0 0.7 copy-done.5
  5.6 0.0 copy-start.6
  5.6 0.7 copy-done.6
  6.3 0.0 copy-start.7
  6.3 0.7 copy-done.7
  6.9 16.1 %sources.1.sent = f32[128,2,384]{2,1,0:T(2,128)S(1)} custom-call(s32[2,152]{1,0:T(2,128)S(1)} %copy-done.4, f32[3,128,128]{2,1,0:T(8,128)S(1)} %copy-done.2, f32[2,128,128]{2,1,0:T(8,128)S(1)} %copy-done.3, s32[1,128]{1,0:T(1,128)S(1)} %bitcast.23, s32[1,128]{1,0:T(1,128)S(1)} %bitcast.22, s32[128,1]{1,0:T(8,128)S(1)} %copy.16.owner_col, s32[1,128]{1,0:T(1,128)S(1)} %bitcast.24), custom_call_target="tpu_custom_call" | custom-call | tf_op jit(solution)/shard_map/sources/pallas_call | solution.py:123
  23.1 0.0 copy-done.1
  23.1 35.9 %exchange.1 = (bf16[2,3,304,256]{3,2,1,0:T(8,128)(2,1)S(1)}, bf16[304,256]{1,0:T(8,128)(2,1)S(1)}) custom-call(f32[128,2,384]{2,1,0:T(2,128)S(1)} %sources.1.sent, f32[304,304]{1,0:T(8,128)S(1)} %copy-done.1), custom_call_target="tpu_custom_call" | custom-call | tf_op jit(solution)/shard_map/exchange/pallas_call | solution.py:268
  59.0 27.5 %translate.1 = f32[304,256]{1,0:T(8,128)S(1)} custom-call(s32[128,256]{1,0:T(8,128)S(1)} %pad_add_fusion.lists, bf16[2,3,304,256]{3,2,1,0:T(8,128)(2,1)S(1)} %get-tuple-element.4.windows, bf16[304,19456]{1,0:T(8,128)(2,1)} %bitcast.25, bf16[304,19456]{1,0:T(8,128)(2,1)} %bitcast.26), custom_call_target="tpu_custom_call" | custom-call | tf_op jit(solution)/shard_map/translate/pallas_call | solution.py:332
  86.5 1.0 %copy.19 = f32[304,1,256]{2,1,0:T(1,128)} copy(f32[304,1,256]{2,0,1:T(8,128)S(1)} %bitcast.21) | data formatting | bytes 622592
  87.6 0.2 copy.17
  87.7 0.5 copy.18
  88.2 0.0 copy-done
  88.2 1.2 %convolution_bitcast_fusion = f32[304,1,32]{0,2,1:T(8,128)} fusion(bf16[304,2432]{1,0:T(8,128)(2,1)S(1)} %copy-done, bf16[304,8,32]{2,1,0:T(8,128)(2,1)S(1)} %copy.18), kind=kOutput, calls=%fused_computation | convolution fusion | flops 47316992 | bytes 1673216 | tf_op jit(solution)/shard_map/dot_general | solution.py:376
  (1 shorter events, 0.0 us)
Async XLA Ops:
  0.6 87.6 %copy-start = (bf16[304,2432]{1,0:T(8,128)(2,1)S(1)}, bf16[304,2432]{1,0:T(8,128)(2,1)}, u32[]{:S(2)}) copy-start(bf16[304,2432]{1,0:T(8,128)(2,1)} %param.20) | copy-start | bytes 4435972
  0.6 22.4 %copy-start.1 = (f32[304,304]{1,0:T(8,128)S(1)}, f32[304,304]{1,0:T(8,128)}, u32[]{:S(2)}) copy-start(f32[304,304]{1,0:T(8,128)} %upward.1) | copy-start | bytes 1108996
  2.5 0.9 %copy-start.2 = (f32[3,128,128]{2,1,0:T(8,128)S(1)}, f32[3,128,128]{2,1,0:T(8,128)}, u32[]{:S(2)}) copy-start(f32[3,128,128]{2,1,0:T(8,128)} %positions.1) | copy-start | bytes 589828
  3.4 0.9 %copy-start.3 = (f32[2,128,128]{2,1,0:T(8,128)S(1)}, f32[2,128,128]{2,1,0:T(8,128)}, u32[]{:S(2)}) copy-start(f32[2,128,128]{2,1,0:T(8,128)} %charges.1) | copy-start | bytes 393220
  4.3 0.7 copy-start.4
  5.0 0.7 copy-start.5
  5.6 0.7 copy-start.6
  6.3 0.7 copy-start.7

commit v3 on v2

v3 whole, which is shorter than its diff:
```python
import functools

import jax
import jax.numpy as jnp
import numpy as np
from jax import lax
from jax.experimental import pallas as pl
from jax.experimental.pallas import tpu as pltpu
from jax.sharding import PartitionSpec as P
from numpy.polynomial import chebyshev, polynomial

GRID = 6
LANES = 384
VM = pl.BlockSpec(memory_space=pltpu.VMEM)
HBM = pl.BlockSpec(memory_space=pltpu.HBM)
SM = pl.BlockSpec(memory_space=pltpu.SMEM)


def surface_index(grid_size):
    indices = np.arange(grid_size)
    lattice = np.stack(np.meshgrid(indices, indices, indices, indexing="ij"), -1).reshape(-1, 3)
    outside = np.any((lattice == 0) | (lattice == grid_size - 1), axis=1)
    return lattice[outside].astype(np.int32)


def node_coordinates(grid_size):
    middle = (grid_size - 1) / 2.0
    return ((np.arange(grid_size) - middle) * (1.5 / middle)).astype(np.float32)


def series(function, degree):
    fitted = chebyshev.Chebyshev.interpolate(function, degree, domain=[1.0, 12.0])
    return [float(value) for value in fitted.convert(kind=polynomial.Polynomial).coef]


HALF_SINE = series(lambda s: np.sin(np.sqrt(s) / 2) / (np.sqrt(s) / 2), 4)
HALF_COSINE = series(lambda s: np.cos(np.sqrt(s) / 2), 5)


def horner(coefficients, s):
    value = coefficients[-1] * s + coefficients[-2]
    for coefficient in coefficients[-3::-1]:
        value = value * s + coefficient
    return value


def waves(s):
    sine = horner(HALF_SINE, s)
    cosine = horner(HALF_COSINE, s)
    sine = sine * cosine
    cosine = cosine * cosine
    cosine = (cosine + cosine) - 1.0
    twice = cosine + cosine
    return (twice * cosine - 1.0) * lax.rsqrt(s), twice * sine


def pieces(value, count=3):
    terms = []
    for _ in range(count):
        terms.append(value.astype(jnp.bfloat16))
        value = value - terms[-1].astype(jnp.float32)
    return terms


def source_sums(table, positions, charges, counts, planes, depths, live_charges, values):
    nodes = node_coordinates(GRID)
    blocks, rows = positions.shape[1:]
    x, y, z = positions[0].T, positions[1].T, positions[2].T
    squares = []
    for node in nodes:
        delta = float(node) - y
        squares.append(delta * delta)
    for i, node in enumerate(nodes):
        delta = float(node) - x
        delta = delta * delta
        for j in range(len(nodes)):
            planes[i * len(nodes) + j] = delta + squares[j]
        delta = float(node) - z
        depths[i] = delta * delta
    live = lax.broadcasted_iota(jnp.int32, (rows, blocks), 0) < counts[...]
    for part in range(2):
        live_charges[part] = jnp.where(live, charges[part].T, 0.0)
    points = table.shape[1]

    def one_point(p, carry):
        plane = table[0, p]
        depth = table[1, p]
        real = imaginary = None
        for chunk in range(rows // 8):
            place = pl.ds(8 * chunk, 8)
            cosine, sine = waves(planes[plane, place, :] + depths[depth, place, :])
            first = live_charges[0, place, :]
            second = live_charges[1, place, :]
            a = cosine * first - sine * second
            b = sine * first + cosine * second
            real = a if real is None else real + a
            imaginary = b if imaginary is None else imaginary + b
        values[pl.ds(p, 1), :] = jnp.sum(real, axis=0, keepdims=True)
        values[pl.ds(points + p, 1), :] = jnp.sum(imaginary, axis=0, keepdims=True)
        return carry

    lax.fori_loop(0, points, one_point, 0)


def fill_slots(values, owners, sent):
    devices, capacity, _ = sent.shape
    blocks = owners.shape[1]
    shape = (blocks, blocks)
    target = jnp.broadcast_to(owners[...].astype(jnp.float32), shape)
    earlier = (target == target.T) & (
        lax.broadcasted_iota(jnp.int32, shape, 0) < lax.broadcasted_iota(jnp.int32, shape, 1)
    )
    rank = jnp.sum(jnp.where(earlier, 1.0, 0.0), axis=0, keepdims=True)
    terms = pieces(values[...])
    device = lax.broadcasted_iota(jnp.int32, (devices, blocks), 0)
    for place in range(capacity):
        pick = jnp.where((device == owners[...]) & (rank == place), 1.0, 0.0).astype(jnp.bfloat16)
        sent[:, place, :] = sum(
            lax.dot_general(pick, term, (((1,), (1,)), ((), ())), preferred_element_type=jnp.float32)
            for term in terms
        )


def raise_arrived(arrived, upward, leaf_count):
    devices, capacity, _ = arrived.shape
    channels = upward.shape[0]
    values = jnp.concatenate([arrived[:, place, :] for place in range(capacity)], axis=0)
    leaf = values[:, channels : channels + 1].astype(jnp.int32)
    members = jnp.where(
        lax.broadcasted_iota(jnp.int32, (devices * capacity, leaf_count), 1) == leaf, 1.0, 0.0
    ).astype(jnp.bfloat16)
    raised = lax.dot_general(
        upward[...],
        values[:, :channels],
        (((1,), (1,)), ((), ())),
        precision=lax.Precision.HIGHEST,
        preferred_element_type=jnp.float32,
    )
    summed = sum(
        jnp.dot(term, members, preferred_element_type=jnp.float32) for term in pieces(raised)
    )
    return summed.astype(jnp.bfloat16)


def parents_of(multipole, child_ops):
    channels, leaf_count = multipole.shape
    family = child_ops.shape[1] // channels
    wide = jnp.broadcast_to(
        multipole.astype(jnp.float32)[:, None, :], (channels, family, leaf_count)
    )
    shape = (channels, family, leaf_count)
    mine = lax.broadcasted_iota(jnp.int32, shape, 2) % family == lax.broadcasted_iota(
        jnp.int32, shape, 1
    )
    children = jnp.where(mine, wide, 0.0).reshape(channels * family, leaf_count)
    spread = jnp.dot(
        child_ops[...], children.astype(jnp.bfloat16), preferred_element_type=jnp.float32
    )
    shape = (leaf_count // family, leaf_count)
    group = jnp.where(
        lax.broadcasted_iota(jnp.int32, shape, 1) // family
        == lax.broadcasted_iota(jnp.int32, shape, 0),
        1.0,
        0.0,
    ).astype(jnp.bfloat16)
    return sum(
        lax.dot_general(group, term, (((1,), (1,)), ((), ())), preferred_element_type=jnp.float32)
        for term in pieces(spread)
    )


def step_kernel(
    table,
    positions_in,
    charges_in,
    counts_in,
    owners_in,
    leaves_in,
    near_in,
    image_in,
    upward_in,
    child_in,
    direct_in,
    mirrored_in,
    potentials,
    parents,
    positions,
    charges,
    counts,
    owners,
    leaves,
    lists,
    upward,
    child_ops,
    operators,
    planes,
    depths,
    live_charges,
    values,
    sent,
    arrived,
    windows,
    gathered,
    input_sem,
    operator_sem,
    send_sem,
    arrive_sem,
    halo_send,
    halo_recv,
):
    box, depth = lax.axis_index("box"), lax.axis_index("depth")
    boxes, slabs = lax.axis_size("box"), lax.axis_size("depth")
    devices, capacity, _ = sent.shape
    channels, leaf_count = potentials.shape
    offsets = near_in.shape[0]
    steps, _, width = operators.shape
    batch = width // channels
    half = steps // 2
    me = box * slabs + depth

    fetches = [
        pltpu.make_async_copy(source, place, input_sem.at[number])
        for number, (source, place) in enumerate(
            [
                (positions_in, positions),
                (charges_in, charges),
                (counts_in, counts),
                (owners_in, owners),
                (leaves_in, leaves),
                (near_in, lists.at[pl.ds(0, offsets)]),
                (image_in, lists.at[pl.ds(offsets, offsets)]),
                (upward_in, upward),
                (child_in, child_ops),
            ]
        )
    ]
    for fetch in fetches:
        fetch.start()
    for step in range(steps):
        pltpu.make_async_copy(
            (direct_in if step < half else mirrored_in).at[
                :, pl.ds(step % half * width, width)
            ],
            operators.at[step],
            operator_sem.at[step],
        ).start()

    def coordinates(device):
        return (device // slabs, lax.rem(device, slabs))

    barrier = pltpu.get_barrier_semaphore()

    def greet(j, carry):
        pl.semaphore_signal(
            barrier,
            inc=1,
            device_id=coordinates(lax.rem(me + j, devices)),
            device_id_type=pl.DeviceIdType.MESH,
        )
        return carry

    lax.fori_loop(1, devices, greet, 0)
    values[...] = jnp.zeros_like(values)
    for fetch in fetches:
        fetch.wait()
    source_sums(table, positions, charges, counts, planes, depths, live_charges, values)
    values[pl.ds(channels, 1), :] = leaves[...].astype(jnp.float32)
    fill_slots(values, owners, sent)
    pl.semaphore_wait(barrier, devices - 1)

    def route(j, carry):
        target = lax.rem(me + j, devices)
        pltpu.make_async_remote_copy(
            src_ref=sent.at[target],
            dst_ref=arrived.at[me],
            send_sem=send_sem,
            recv_sem=arrive_sem,
            device_id=coordinates(target),
            device_id_type=pl.DeviceIdType.MESH,
        ).start()
        return carry

    lax.fori_loop(1, devices, route, 0)
    arrived[me] = sent[me]
    others = pl.ds(0, devices - 1)
    every = pltpu.make_async_remote_copy(
        src_ref=sent.at[others],
        dst_ref=arrived.at[others],
        send_sem=send_sem,
        recv_sem=arrive_sem,
        device_id=(lax.rem(box + 1, boxes), depth),
        device_id_type=pl.DeviceIdType.MESH,
    )
    every.wait_send()
    every.wait_recv()
    windows[0, 1] = raise_arrived(arrived, upward, leaf_count)

    def copy(number, source, place, device):
        return pltpu.make_async_remote_copy(
            src_ref=windows.at[source],
            dst_ref=windows.at[place],
            send_sem=halo_send.at[number],
            recv_sem=halo_recv.at[number],
            device_id=device,
            device_id_type=pl.DeviceIdType.MESH,
        )

    def beside(number, slab):
        to_right = copy(number, (slab, 1), (slab, 0), (box + 1, depth))
        to_left = copy(number + 1, (slab, 1), (slab, 2), (box - 1, depth))
        return to_right, to_left

    mirror = copy(4, (0, 1), (1, 1), (box, slabs - 1 - depth))
    direct, image = beside(0, 0), beside(2, 1)
    has_left, has_right = box > 0, box < boxes - 1
    blank = jnp.zeros((channels, leaf_count), jnp.bfloat16)

    def start(pair):
        @pl.when(has_right)
        def _():
            pair[0].start()

        @pl.when(has_left)
        def _():
            pair[1].start()

    def receive(pair):
        @pl.when(has_left)
        def _():
            pair[0].wait_recv()

        @pl.when(has_right)
        def _():
            pair[1].wait_recv()

    def sent_off(pair):
        @pl.when(has_right)
        def _():
            pair[0].wait_send()

        @pl.when(has_left)
        def _():
            pair[1].wait_send()

    start(direct)
    mirror.start()

    @pl.when(jnp.logical_not(has_left))
    def _():
        windows[0, 0] = blank
        windows[1, 0] = blank

    @pl.when(jnp.logical_not(has_right))
    def _():
        windows[0, 2] = blank
        windows[1, 2] = blank

    parents[...] = parents_of(windows[0, 1], child_ops)
    potentials[...] = jnp.zeros_like(potentials)
    receive(direct)
    row = lax.broadcasted_iota(jnp.int32, (leaf_count, leaf_count), 0)

    def translate(step, carry):
        @pl.when(step == half // 2)
        def _():
            mirror.wait_recv()
            start(image)

        @pl.when(step == half)
        def _():
            receive(image)

        pltpu.make_async_copy(
            direct_in.at[:, pl.ds(0, width)], operators.at[step], operator_sem.at[step]
        ).wait()
        slab = step // half
        window = jnp.concatenate([windows[slab, part] for part in range(3)], axis=1)
        for o in range(batch):
            chosen = lists[step * batch + o]
            hot = jnp.concatenate(
                [
                    jnp.where(row == chosen - part * leaf_count, 1.0, 0.0).astype(jnp.bfloat16)
                    for part in range(3)
                ],
                axis=0,
            )
            picked = jnp.dot(window, hot, preferred_element_type=jnp.float32)
            gathered[pl.ds(o * channels, channels), :] = picked.astype(jnp.bfloat16)
        potentials[...] += jnp.dot(
            operators[step], gathered[...], preferred_element_type=jnp.float32
        )
        return carry

    lax.fori_loop(0, steps, translate, 0)
    sent_off(direct)
    sent_off(image)
    mirror.wait_send()


def local(
    positions,
    charges,
    counts,
    owners,
    leaves,
    near_lists,
    image_lists,
    upward,
    child_ops,
    direct_ops,
    image_ops,
):
    devices = lax.axis_size("box") * lax.axis_size("depth")
    blocks, rows = positions.shape[1:]
    capacity = 2 * blocks // devices
    offsets, _, leaf_count = near_lists.shape
    channels = upward.shape[0]
    index = surface_index(GRID)
    table = jnp.asarray(np.stack([index[:, 0] * GRID + index[:, 1], index[:, 2]]))
    batch = 16
    steps = 2 * offsets // batch
    parent_count = leaf_count * channels // child_ops.shape[1]

    def scratch(*shape, dtype=jnp.float32):
        return pltpu.VMEM(shape, dtype)

    potentials, parents = pl.pallas_call(
        step_kernel,
        out_shape=(
            jax.ShapeDtypeStruct((channels, leaf_count), jnp.float32),
            jax.ShapeDtypeStruct((parent_count, channels), jnp.float32),
        ),
        in_specs=[SM] + [HBM] * 11,
        out_specs=(VM, VM),
        scratch_shapes=[
            scratch(*positions.shape),
            scratch(*charges.shape),
            scratch(1, blocks, dtype=jnp.int32),
            scratch(1, blocks, dtype=jnp.int32),
            scratch(1, blocks, dtype=jnp.int32),
            scratch(2 * offsets, 1, leaf_count, dtype=jnp.int32),
            scratch(*upward.shape),
            scratch(*child_ops.shape, dtype=jnp.bfloat16),
            scratch(steps, channels, batch * channels, dtype=jnp.bfloat16),
            scratch(GRID * GRID, rows, blocks),
            scratch(GRID, rows, blocks),
            scratch(2, rows, blocks),
            scratch(LANES, blocks),
            scratch(devices, capacity, LANES),
            scratch(devices, capacity, LANES),
            scratch(2, 3, channels, leaf_count, dtype=jnp.bfloat16),
            scratch(batch * channels, leaf_count, dtype=jnp.bfloat16),
            pltpu.SemaphoreType.DMA((9,)),
            pltpu.SemaphoreType.DMA((steps,)),
            pltpu.SemaphoreType.DMA,
            pltpu.SemaphoreType.DMA,
            pltpu.SemaphoreType.DMA((5,)),
            pltpu.SemaphoreType.DMA((5,)),
        ],
        compiler_params=pltpu.CompilerParams(
            vmem_limit_bytes=56 << 20, has_side_effects=True, collective_id=0
        ),
        name="step",
    )(
        table,
        positions,
        charges,
        counts.reshape(1, blocks),
        owners.reshape(1, blocks),
        leaves.reshape(1, blocks),
        near_lists,
        image_lists,
        upward,
        child_ops,
        direct_ops.T,
        image_ops.T,
    )
    return (potentials[:, None, :], parents.T[:, None, :])


def solution(mesh):
    return jax.shard_map(
        local,
        mesh=mesh,
        in_specs=(
            P(None, ("box", "depth"), None),
            P(None, ("box", "depth"), None),
            P(("box", "depth")),
            P(("box", "depth"), None),
            P(("box", "depth")),
            P(None, "depth", "box"),
            P(None, "depth", "box"),
            P(),
            P(),
            P(),
            P(),
        ),
        out_specs=(P(None, "depth", "box"), P(None, "depth", "box")),
        check_vma=False,
    )
```

time: 89.6 us -> 76.1 us (0.85)
  Pallas kernels: 79.6 us -> 71.5 us
  local copies, waits for them, and re-layouts: 7.92 us -> 3.43 us
  matrix products: 1.17 us -> 0 us
    pallas_call x3 -> x1, Pallas kernels: 79.6 us -> 71.5 us  [local(): pl.pallas_call(step_kernel, out_shape=(jax.ShapeDtypeStruct((channels, le...]
    unnamed x19 -> x2, local copies, waits for them, and re-layouts: 7.31 us -> 3.43 us
    dot_general x1 -> x0, matrix products: 1.17 us -> none  [local(): parents = jnp.dot(child_ops, children, preferred_element_type=jnp.float32)]
where the time goes in v3:
time: 76.1 us; the launch traced here: 75.5 us
  Pallas kernels  71.5 us (94%)
  local copies, waits for them, and re-layouts  3.43 us (5%)
    pallas_call x1, Pallas kernels, local(): pl.pallas_call(step_kernel, out_shape=(jax.ShapeDtypeStruct((channels, le...  71.5 us
    unnamed x2, local copies, waits for them, and re-layouts  3.43 us

profile of v3, /device:TPU:1, one launch (start us, length us, event | category | flops | bytes accessed | tf_op | source)
XLA Modules:
  0.0 75.5 jit_solution(6128825487476212417)
XLA Ops:
  0.6 71.5 %step.1 = (f32[304,256]{1,0:T(8,128)}, f32[32,304]{1,0:T(8,128)}) custom-call(s32[2,152]{1,0:T(2,128)} %constant.2.clone.table, f32[3,128,128]{2,1,0:T(8,128)} %positions_in.1, f32[2,128,128]{2,1,0:T(8,128)} %charges_in.1, s32[1,128]{1,0:T(1,128)} %bitcast.13, s32[1,128]{1,0:T(1,128)} %bitcast.14, s32[1,128]{1,0:T(1,128)} %bitcast.15, ...), custom_call_target="tpu_custom_call" | custom-call | tf_op jit(solution)/shard_map/step/pallas_call | solution.py:427
  72.1 2.0 %copy.14 = f32[304,1,256]{2,1,0:T(1,128)} copy(f32[304,1,256]{2,0,1:T(8,128)} %bitcast.11) | data formatting | bytes 622592
  74.1 1.4 %copy.16 = f32[304,1,32]{0,2,1:T(8,128)} copy(f32[304,1,32]{0,2,1:T(8,128)} %bitcast.12) | data formatting | bytes 77824

commit v4 on v3

--- a/solution.py
+++ b/solution.py
@@ -10,7 +10,6 @@
 from numpy.polynomial import chebyshev, polynomial
 
 GRID = 6
-LANES = 384
 VM = pl.BlockSpec(memory_space=pltpu.VMEM)
 HBM = pl.BlockSpec(memory_space=pltpu.HBM)
 SM = pl.BlockSpec(memory_space=pltpu.SMEM)
@@ -37,21 +36,22 @@
 HALF_COSINE = series(lambda s: np.cos(np.sqrt(s) / 2), 5)
 
 
-def horner(coefficients, s):
-    value = coefficients[-1] * s + coefficients[-2]
+SCALE = 2.0 * HALF_SINE[-1] * HALF_COSINE[-1]
+
+
+def monic(coefficients, s):
+    value = s + coefficients[-2] / coefficients[-1]
     for coefficient in coefficients[-3::-1]:
-        value = value * s + coefficient
+        value = value * s + coefficient / coefficients[-1]
     return value
 
 
 def waves(s):
-    sine = horner(HALF_SINE, s)
-    cosine = horner(HALF_COSINE, s)
+    sine = monic(HALF_SINE, s)
+    cosine = monic(HALF_COSINE, s)
     sine = sine * cosine
-    cosine = cosine * cosine
-    cosine = (cosine + cosine) - 1.0
-    twice = cosine + cosine
-    return (twice * cosine - 1.0) * lax.rsqrt(s), twice * sine
+    cosine = cosine * cosine * (2.0 * HALF_COSINE[-1] ** 2) - 1.0
+    return (cosine * cosine - 0.5) * lax.rsqrt(s), sine * cosine
 
 
 def pieces(value, count=3):
@@ -79,7 +79,9 @@
         depths[i] = delta * delta
     live = lax.broadcasted_iota(jnp.int32, (rows, blocks), 0) < counts[...]
     for part in range(2):
-        live_charges[part] = jnp.where(live, charges[part].T, 0.0)
+        charge = jnp.where(live, charges[part].T, 0.0)
+        live_charges[part] = 2.0 * charge
+        live_charges[2 + part] = SCALE * charge
     points = table.shape[1]
 
     def one_point(p, carry):
@@ -89,49 +91,66 @@
         for chunk in range(rows // 8):
             place = pl.ds(8 * chunk, 8)
             cosine, sine = waves(planes[plane, place, :] + depths[depth, place, :])
-            first = live_charges[0, place, :]
-            second = live_charges[1, place, :]
-            a = cosine * first - sine * second
-            b = sine * first + cosine * second
+            a = cosine * live_charges[0, place, :] - sine * live_charges[3, place, :]
+            b = sine * live_charges[2, place, :] + cosine * live_charges[1, place, :]
             real = a if real is None else real + a
             imaginary = b if imaginary is None else imaginary + b
         values[pl.ds(p, 1), :] = jnp.sum(real, axis=0, keepdims=True)
         values[pl.ds(points + p, 1), :] = jnp.sum(imaginary, axis=0, keepdims=True)
         return carry
 
-    lax.fori_loop(0, points, one_point, 0)
-
-
-def fill_slots(values, owners, sent):
-    devices, capacity, _ = sent.shape
-    blocks = owners.shape[1]
+    lax.fori_loop(0, points, one_point, 0, unroll=4)
+
+
+def fill_slots(values, owners, leaves, sent, capacity):
+    devices, _, width = sent.shape
+    channels, blocks = values.shape
     shape = (blocks, blocks)
     target = jnp.broadcast_to(owners[...].astype(jnp.float32), shape)
     earlier = (target == target.T) & (
         lax.broadcasted_iota(jnp.int32, shape, 0) < lax.broadcasted_iota(jnp.int32, shape, 1)
     )
     rank = jnp.sum(jnp.where(earlier, 1.0, 0.0), axis=0, keepdims=True)
-    terms = pieces(values[...])
     device = lax.broadcasted_iota(jnp.int32, (devices, blocks), 0)
+    spare = width - capacity * channels
+    place_row = lax.broadcasted_iota(jnp.int32, (spare, blocks), 0)
+    leaf = jnp.broadcast_to(leaves[...].astype(jnp.float32), (spare, blocks))
+    filled = None
     for place in range(capacity):
         pick = jnp.where((device == owners[...]) & (rank == place), 1.0, 0.0).astype(jnp.bfloat16)
-        sent[:, place, :] = sum(
-            lax.dot_general(pick, term, (((1,), (1,)), ((), ())), preferred_element_type=jnp.float32)
-            for term in terms
+        column = jnp.concatenate(
+            [
+                values[...] if other == place else jnp.zeros((channels, blocks), jnp.float32)
+                for other in range(capacity)
+            ]
+            + [jnp.where(place_row == place, leaf, 0.0)],
+            axis=0,
         )
-
-
-def raise_arrived(arrived, upward, leaf_count):
-    devices, capacity, _ = arrived.shape
+        for term in pieces(column):
+            part = lax.dot_general(
+                pick, term, (((1,), (1,)), ((), ())), preferred_element_type=jnp.float32
+            )
+            filled = part if filled is None else filled + part
+    sent[:, 0, :] = filled
+
+
+def raise_arrived(arrived, upward, leaf_count, capacity):
+    devices = arrived.shape[0]
     channels = upward.shape[0]
-    values = jnp.concatenate([arrived[:, place, :] for place in range(capacity)], axis=0)
-    leaf = values[:, channels : channels + 1].astype(jnp.int32)
+    rows = arrived[:, 0, :]
+    first = capacity * channels
+    values = jnp.concatenate(
+        [rows[:, place * channels : (place + 1) * channels] for place in range(capacity)], axis=0
+    )
+    leaf = jnp.concatenate(
+        [rows[:, first + place : first + place + 1] for place in range(capacity)], axis=0
+    ).astype(jnp.int32)
     members = jnp.where(
         lax.broadcasted_iota(jnp.int32, (devices * capacity, leaf_count), 1) == leaf, 1.0, 0.0
     ).astype(jnp.bfloat16)
     raised = lax.dot_general(
         upward[...],
-        values[:, :channels],
+        values,
         (((1,), (1,)), ((), ())),
         precision=lax.Precision.HIGHEST,
         preferred_element_type=jnp.float32,
@@ -210,8 +229,9 @@
 ):
     box, depth = lax.axis_index("box"), lax.axis_index("depth")
     boxes, slabs = lax.axis_size("box"), lax.axis_size("depth")
-    devices, capacity, _ = sent.shape
+    devices = sent.shape[0]
     channels, leaf_count = potentials.shape
+    capacity = sent.shape[2] // channels
     offsets = near_in.shape[0]
     steps, _, width = operators.shape
     batch = width // channels
@@ -234,7 +254,34 @@
             ]
         )
     ]
-    for fetch in fetches:
+    for fetch in fetches[:5]:
+        fetch.start()
+    barrier = pltpu.get_barrier_semaphore()
+    columns = [lax.rem(depth + ahead, slabs) for ahead in range(slabs)]
+
+    def every_device(send):
+        def one_row(ahead, carry):
+            target_box = lax.rem(box + ahead, boxes)
+            for column in columns:
+                send(target_box, column)
+            return carry
+
+        for column in columns[1:]:
+            send(box, column)
+        lax.fori_loop(1, boxes, one_row, 0)
+
+    def greet(target_box, target_depth):
+        pl.semaphore_signal(
+            barrier,
+            inc=1,
+            device_id=(target_box, target_depth),
+            device_id_type=pl.DeviceIdType.MESH,
+        )
+
+    every_device(greet)
+    for fetch in fetches[:5]:
+        fetch.wait()
+    for fetch in fetches[5:]:
         fetch.start()
     for step in range(steps):
         pltpu.make_async_copy(
@@ -244,43 +291,21 @@
             operators.at[step],
             operator_sem.at[step],
         ).start()
-
-    def coordinates(device):
-        return (device // slabs, lax.rem(device, slabs))
-
-    barrier = pltpu.get_barrier_semaphore()
-
-    def greet(j, carry):
-        pl.semaphore_signal(
-            barrier,
-            inc=1,
-            device_id=coordinates(lax.rem(me + j, devices)),
-            device_id_type=pl.DeviceIdType.MESH,
-        )
-        return carry
-
-    lax.fori_loop(1, devices, greet, 0)
-    values[...] = jnp.zeros_like(values)
-    for fetch in fetches:
-        fetch.wait()
     source_sums(table, positions, charges, counts, planes, depths, live_charges, values)
-    values[pl.ds(channels, 1), :] = leaves[...].astype(jnp.float32)
-    fill_slots(values, owners, sent)
+    fill_slots(values, owners, leaves, sent, capacity)
     pl.semaphore_wait(barrier, devices - 1)
 
-    def route(j, carry):
-        target = lax.rem(me + j, devices)
+    def route(target_box, target_depth):
         pltpu.make_async_remote_copy(
-            src_ref=sent.at[target],
+            src_ref=sent.at[target_box * slabs + target_depth],
             dst_ref=arrived.at[me],
             send_sem=send_sem,
             recv_sem=arrive_sem,
-            device_id=coordinates(target),
+            device_id=(target_box, target_depth),
             device_id_type=pl.DeviceIdType.MESH,
         ).start()
-        return carry
-
-    lax.fori_loop(1, devices, route, 0)
+
+    every_device(route)
     arrived[me] = sent[me]
     others = pl.ds(0, devices - 1)
     every = pltpu.make_async_remote_copy(
@@ -291,9 +316,11 @@
         device_id=(lax.rem(box + 1, boxes), depth),
         device_id_type=pl.DeviceIdType.MESH,
     )
+    for fetch in fetches[5:]:
+        fetch.wait()
     every.wait_send()
     every.wait_recv()
-    windows[0, 1] = raise_arrived(arrived, upward, leaf_count)
+    windows[0, 1] = raise_arrived(arrived, upward, leaf_count, capacity)
 
     def copy(number, source, place, device):
         return pltpu.make_async_remote_copy(
@@ -419,6 +446,7 @@
     table = jnp.asarray(np.stack([index[:, 0] * GRID + index[:, 1], index[:, 2]]))
     batch = 16
     steps = 2 * offsets // batch
+    width = -(-capacity * (channels + 1) // 128) * 128
     parent_count = leaf_count * channels // child_ops.shape[1]
 
     def scratch(*shape, dtype=jnp.float32):
@@ -444,10 +472,10 @@
             scratch(steps, channels, batch * channels, dtype=jnp.bfloat16),
             scratch(GRID * GRID, rows, blocks),
             scratch(GRID, rows, blocks),
-            scratch(2, rows, blocks),
-            scratch(LANES, blocks),
-            scratch(devices, capacity, LANES),
-            scratch(devices, capacity, LANES),
+            scratch(4, rows, blocks),
+            scratch(channels, blocks),
+            scratch(devices, 1, width),
+            scratch(devices, 1, width),
             scratch(2, 3, channels, leaf_count, dtype=jnp.bfloat16),
             scratch(batch * channels, leaf_count, dtype=jnp.bfloat16),
             pltpu.SemaphoreType.DMA((9,)),

time: 76.1 us -> 65.8 us (0.86)
  Pallas kernels: 71.5 us -> 61.5 us
    pallas_call x1, Pallas kernels: 71.5 us -> 61.5 us  [local(): pl.pallas_call(step_kernel, out_shape=(jax.ShapeDtypeStruct((channels, le...]
where the time goes in v4:
time: 65.8 us; the launch traced here: 65.5 us
  Pallas kernels  61.5 us (93%)
  local copies, waits for them, and re-layouts  3.43 us (5%)
    pallas_call x1, Pallas kernels, local(): pl.pallas_call(step_kernel, out_shape=(jax.ShapeDtypeStruct((channels, le...  61.5 us
    unnamed x2, local copies, waits for them, and re-layouts  3.43 us

profile of v4, /device:TPU:1, one launch (start us, length us, event | category | flops | bytes accessed | tf_op | source)
XLA Modules:
  0.0 65.5 jit_solution(4863008311134277378)
XLA Ops:
  0.6 61.5 %step.1 = (f32[304,256]{1,0:T(8,128)}, f32[32,304]{1,0:T(8,128)}) custom-call(s32[2,152]{1,0:T(2,128)} %constant.2.clone.table, f32[3,128,128]{2,1,0:T(8,128)} %positions_in.1, f32[2,128,128]{2,1,0:T(8,128)} %charges_in.1, s32[1,128]{1,0:T(1,128)} %bitcast.13, s32[1,128]{1,0:T(1,128)} %bitcast.14, s32[1,128]{1,0:T(1,128)} %bitcast.15, ...), custom_call_target="tpu_custom_call" | custom-call | tf_op jit(solution)/shard_map/step/pallas_call | solution.py:455
  62.1 2.0 %copy.14 = f32[304,1,256]{2,1,0:T(1,128)} copy(f32[304,1,256]{2,0,1:T(8,128)} %bitcast.11) | data formatting | bytes 622592
  64.1 1.4 %copy.16 = f32[304,1,32]{0,2,1:T(8,128)} copy(f32[304,1,32]{0,2,1:T(8,128)} %bitcast.12) | data formatting | bytes 77824

commit v5 on v4

--- a/solution.py
+++ b/solution.py
@@ -62,7 +62,7 @@
     return terms
 
 
-def source_sums(table, positions, charges, counts, planes, depths, live_charges, values):
+def prepare_sources(positions, charges, counts, planes, depths, live_charges):
     nodes = node_coordinates(GRID)
     blocks, rows = positions.shape[1:]
     x, y, z = positions[0].T, positions[1].T, positions[2].T
@@ -82,35 +82,36 @@
         charge = jnp.where(live, charges[part].T, 0.0)
         live_charges[part] = 2.0 * charge
         live_charges[2 + part] = SCALE * charge
-    points = table.shape[1]
-
-    def one_point(p, carry):
-        plane = table[0, p]
-        depth = table[1, p]
-        real = imaginary = None
-        for chunk in range(rows // 8):
-            place = pl.ds(8 * chunk, 8)
-            cosine, sine = waves(planes[plane, place, :] + depths[depth, place, :])
-            a = cosine * live_charges[0, place, :] - sine * live_charges[3, place, :]
-            b = sine * live_charges[2, place, :] + cosine * live_charges[1, place, :]
-            real = a if real is None else real + a
-            imaginary = b if imaginary is None else imaginary + b
-        values[pl.ds(p, 1), :] = jnp.sum(real, axis=0, keepdims=True)
-        values[pl.ds(points + p, 1), :] = jnp.sum(imaginary, axis=0, keepdims=True)
-        return carry
-
-    lax.fori_loop(0, points, one_point, 0, unroll=4)
-
-
-def fill_slots(values, owners, leaves, sent, capacity):
-    devices, _, width = sent.shape
-    channels, blocks = values.shape
+
+
+def sum_point(table, planes, depths, live_charges, values, first, p):
+    plane = table[0, first + p]
+    depth = table[1, first + p]
+    real = imaginary = None
+    for chunk in range(planes.shape[1] // 8):
+        place = pl.ds(8 * chunk, 8)
+        cosine, sine = waves(planes[plane, place, :] + depths[depth, place, :])
+        a = cosine * live_charges[0, place, :] - sine * live_charges[3, place, :]
+        b = sine * live_charges[2, place, :] + cosine * live_charges[1, place, :]
+        real = a if real is None else real + a
+        imaginary = b if imaginary is None else imaginary + b
+    values[pl.ds(p, 1), :] = jnp.sum(real, axis=0, keepdims=True)
+    values[pl.ds(values.shape[0] // 2 + p, 1), :] = jnp.sum(imaginary, axis=0, keepdims=True)
+
+
+def ranks(owners):
+    blocks = owners.shape[1]
     shape = (blocks, blocks)
     target = jnp.broadcast_to(owners[...].astype(jnp.float32), shape)
     earlier = (target == target.T) & (
         lax.broadcasted_iota(jnp.int32, shape, 0) < lax.broadcasted_iota(jnp.int32, shape, 1)
     )
-    rank = jnp.sum(jnp.where(earlier, 1.0, 0.0), axis=0, keepdims=True)
+    return jnp.sum(jnp.where(earlier, 1.0, 0.0), axis=0, keepdims=True)
+
+
+def fill_slots(values, owners, rank, leaves, sent, capacity):
+    devices, _, width = sent.shape
+    channels, blocks = values.shape
     device = lax.broadcasted_iota(jnp.int32, (devices, blocks), 0)
     spare = width - capacity * channels
     place_row = lax.broadcasted_iota(jnp.int32, (spare, blocks), 0)
@@ -134,27 +135,35 @@
     sent[:, 0, :] = filled
 
 
-def raise_arrived(arrived, upward, leaf_count, capacity):
-    devices = arrived.shape[0]
-    channels = upward.shape[0]
+def raise_part(arrived, upward, capacity, first, count):
     rows = arrived[:, 0, :]
-    first = capacity * channels
+    channels = 2 * count
     values = jnp.concatenate(
         [rows[:, place * channels : (place + 1) * channels] for place in range(capacity)], axis=0
     )
+    points = upward.shape[1] // 2
+    columns = jnp.concatenate(
+        [upward[:, first : first + count], upward[:, points + first : points + first + count]],
+        axis=1,
+    )
+    return lax.dot_general(
+        columns,
+        values,
+        (((1,), (1,)), ((), ())),
+        precision=lax.Precision.HIGHEST,
+        preferred_element_type=jnp.float32,
+    )
+
+
+def add_up(raised, arrived, capacity, count, leaf_count):
+    rows = arrived[:, 0, :]
+    first = capacity * 2 * count
     leaf = jnp.concatenate(
         [rows[:, first + place : first + place + 1] for place in range(capacity)], axis=0
     ).astype(jnp.int32)
     members = jnp.where(
-        lax.broadcasted_iota(jnp.int32, (devices * capacity, leaf_count), 1) == leaf, 1.0, 0.0
+        lax.broadcasted_iota(jnp.int32, (leaf.shape[0], leaf_count), 1) == leaf, 1.0, 0.0
     ).astype(jnp.bfloat16)
-    raised = lax.dot_general(
-        upward[...],
-        values,
-        (((1,), (1,)), ((), ())),
-        precision=lax.Precision.HIGHEST,
-        preferred_element_type=jnp.float32,
-    )
     summed = sum(
         jnp.dot(term, members, preferred_element_type=jnp.float32) for term in pieces(raised)
     )
@@ -215,9 +224,12 @@
     planes,
     depths,
     live_charges,
-    values,
-    sent,
-    arrived,
+    early_values,
+    late_values,
+    early_sent,
+    late_sent,
+    early_arrived,
+    late_arrived,
     windows,
     gathered,
     input_sem,
@@ -229,9 +241,10 @@
 ):
     box, depth = lax.axis_index("box"), lax.axis_index("depth")
     boxes, slabs = lax.axis_size("box"), lax.axis_size("depth")
-    devices = sent.shape[0]
+    devices = early_sent.shape[0]
+    early, late = early_values.shape[0] // 2, late_values.shape[0] // 2
     channels, leaf_count = potentials.shape
-    capacity = sent.shape[2] // channels
+    capacity = early_sent.shape[2] // (2 * early)
     offsets = near_in.shape[0]
     steps, _, width = operators.shape
     batch = width // channels
@@ -259,16 +272,21 @@
     barrier = pltpu.get_barrier_semaphore()
     columns = [lax.rem(depth + ahead, slabs) for ahead in range(slabs)]
 
-    def every_device(send):
-        def one_row(ahead, carry):
-            target_box = lax.rem(box + ahead, boxes)
-            for column in columns:
-                send(target_box, column)
-            return carry
-
+    def own_row(send):
         for column in columns[1:]:
             send(box, column)
-        lax.fori_loop(1, boxes, one_row, 0)
+
+    def one_row(ahead, send):
+        target_box = lax.rem(box + ahead, boxes)
+        for column in columns:
+            send(target_box, column)
+
+    def other_rows(send):
+        def body(ahead, carry):
+            one_row(ahead, send)
+            return carry
+
+        lax.fori_loop(1, boxes, body, 0)
 
     def greet(target_box, target_depth):
         pl.semaphore_signal(
@@ -278,7 +296,8 @@
             device_id_type=pl.DeviceIdType.MESH,
         )
 
-    every_device(greet)
+    own_row(greet)
+    other_rows(greet)
     for fetch in fetches[:5]:
         fetch.wait()
     for fetch in fetches[5:]:
@@ -291,36 +310,74 @@
             operators.at[step],
             operator_sem.at[step],
         ).start()
-    source_sums(table, positions, charges, counts, planes, depths, live_charges, values)
-    fill_slots(values, owners, leaves, sent, capacity)
+    prepare_sources(positions, charges, counts, planes, depths, live_charges)
+    rank = ranks(owners)
+
+    def early_point(p, carry):
+        sum_point(table, planes, depths, live_charges, early_values, 0, p)
+        return carry
+
+    lax.fori_loop(0, early, early_point, 0, unroll=4)
+    fill_slots(early_values, owners, rank, leaves, early_sent, capacity)
     pl.semaphore_wait(barrier, devices - 1)
 
-    def route(target_box, target_depth):
-        pltpu.make_async_remote_copy(
-            src_ref=sent.at[target_box * slabs + target_depth],
-            dst_ref=arrived.at[me],
-            send_sem=send_sem,
-            recv_sem=arrive_sem,
-            device_id=(target_box, target_depth),
+    def route(number, sent, arrived):
+        def send(target_box, target_depth):
+            pltpu.make_async_remote_copy(
+                src_ref=sent.at[target_box * slabs + target_depth],
+                dst_ref=arrived.at[me],
+                send_sem=send_sem.at[number],
+                recv_sem=arrive_sem.at[number],
+                device_id=(target_box, target_depth),
+                device_id_type=pl.DeviceIdType.MESH,
+            ).start()
+
+        return send
+
+    def all_routed(number, sent, arrived):
+        others = pl.ds(0, devices - 1)
+        return pltpu.make_async_remote_copy(
+            src_ref=sent.at[others],
+            dst_ref=arrived.at[others],
+            send_sem=send_sem.at[number],
+            recv_sem=arrive_sem.at[number],
+            device_id=(lax.rem(box + 1, boxes), depth),
             device_id_type=pl.DeviceIdType.MESH,
-        ).start()
-
-    every_device(route)
-    arrived[me] = sent[me]
-    others = pl.ds(0, devices - 1)
-    every = pltpu.make_async_remote_copy(
-        src_ref=sent.at[others],
-        dst_ref=arrived.at[others],
-        send_sem=send_sem,
-        recv_sem=arrive_sem,
-        device_id=(lax.rem(box + 1, boxes), depth),
-        device_id_type=pl.DeviceIdType.MESH,
-    )
+        )
+
+    early_send = route(0, early_sent, early_arrived)
+    late_send = route(1, late_sent, late_arrived)
+    early_all = all_routed(0, early_sent, early_arrived)
+    late_all = all_routed(1, late_sent, late_arrived)
+    own_row(early_send)
+
+    def late_points(pair):
+        for p in range(2):
+            sum_point(table, planes, depths, live_charges, late_values, early, 2 * pair + p)
+
+    def late_and_send(pair, carry):
+        late_points(pair)
+        one_row(pair + 1, early_send)
+        return carry
+
+    def late_only(pair, carry):
+        late_points(pair)
+        return carry
+
+    lax.fori_loop(0, boxes - 1, late_and_send, 0)
+    lax.fori_loop(boxes - 1, late // 2, late_only, 0)
+    fill_slots(late_values, owners, rank, leaves, late_sent, capacity)
+    own_row(late_send)
+    other_rows(late_send)
+    early_arrived[me] = early_sent[me]
+    late_arrived[me] = late_sent[me]
     for fetch in fetches[5:]:
         fetch.wait()
-    every.wait_send()
-    every.wait_recv()
-    windows[0, 1] = raise_arrived(arrived, upward, leaf_count, capacity)
+    early_all.wait_recv()
+    raised = raise_part(early_arrived, upward, capacity, 0, early)
+    late_all.wait_recv()
+    raised += raise_part(late_arrived, upward, capacity, early, late)
+    windows[0, 1] = add_up(raised, late_arrived, capacity, late, leaf_count)
 
     def copy(number, source, place, device):
         return pltpu.make_async_remote_copy(
@@ -419,6 +476,8 @@
         return carry
 
     lax.fori_loop(0, steps, translate, 0)
+    early_all.wait_send()
+    late_all.wait_send()
     sent_off(direct)
     sent_off(image)
     mirror.wait_send()
@@ -444,9 +503,12 @@
     channels = upward.shape[0]
     index = surface_index(GRID)
     table = jnp.asarray(np.stack([index[:, 0] * GRID + index[:, 1], index[:, 2]]))
-    batch = 16
+    batch = 32
     steps = 2 * offsets // batch
-    width = -(-capacity * (channels + 1) // 128) * 128
+    points = channels // 2
+    early = points * 11 // 16 // 8 * 8
+    parts = (early, points - early)
+    widths = [-(-capacity * (2 * part + 1) // 128) * 128 for part in parts]
     parent_count = leaf_count * channels // child_ops.shape[1]
 
     def scratch(*shape, dtype=jnp.float32):
@@ -473,15 +535,14 @@
             scratch(GRID * GRID, rows, blocks),
             scratch(GRID, rows, blocks),
             scratch(4, rows, blocks),
-            scratch(channels, blocks),
-            scratch(devices, 1, width),
-            scratch(devices, 1, width),
+            *[scratch(2 * part, blocks) for part in parts],
+            *[scratch(devices, 1, width) for width in widths * 2],
             scratch(2, 3, channels, leaf_count, dtype=jnp.bfloat16),
             scratch(batch * channels, leaf_count, dtype=jnp.bfloat16),
             pltpu.SemaphoreType.DMA((9,)),
             pltpu.SemaphoreType.DMA((steps,)),
-            pltpu.SemaphoreType.DMA,
-            pltpu.SemaphoreType.DMA,
+            pltpu.SemaphoreType.DMA((2,)),
+            pltpu.SemaphoreType.DMA((2,)),
             pltpu.SemaphoreType.DMA((5,)),
             pltpu.SemaphoreType.DMA((5,)),
         ],

time: 65.8 us -> 64 us (0.973)
  Pallas kernels: 61.5 us -> 59.7 us
    pallas_call x1, Pallas kernels: 61.5 us -> 59.7 us  [local(): pl.pallas_call(step_kernel, out_shape=(jax.ShapeDtypeStruct((channels, le...]
where the time goes in v5:
time: 64 us; the launch traced here: 63.8 us
  Pallas kernels  59.7 us (93%)
  local copies, waits for them, and re-layouts  3.43 us (5%)
  between operations  0.64 us (1%)
    pallas_call x1, Pallas kernels, local(): pl.pallas_call(step_kernel, out_shape=(jax.ShapeDtypeStruct((channels, le...  59.7 us
    unnamed x2, local copies, waits for them, and re-layouts  3.43 us

profile of v5, /device:TPU:1, one launch (start us, length us, event | category | flops | bytes accessed | tf_op | source)
XLA Modules:
  0.0 63.8 jit_solution(10823272192348143859)
XLA Ops:
  0.6 59.7 %step.1 = (f32[304,256]{1,0:T(8,128)}, f32[32,304]{1,0:T(8,128)}) custom-call(s32[2,152]{1,0:T(2,128)} %constant.2.clone.table, f32[3,128,128]{2,1,0:T(8,128)} %positions_in.1, f32[2,128,128]{2,1,0:T(8,128)} %charges_in.1, s32[1,128]{1,0:T(1,128)} %bitcast.13, s32[1,128]{1,0:T(1,128)} %bitcast.14, s32[1,128]{1,0:T(1,128)} %bitcast.15, ...), custom_call_target="tpu_custom_call" | custom-call | tf_op jit(solution)/shard_map/step/pallas_call | solution.py:517
  60.4 2.0 %copy.14 = f32[304,1,256]{2,1,0:T(1,128)} copy(f32[304,1,256]{2,0,1:T(8,128)} %bitcast.11) | data formatting | bytes 622592
  62.4 1.4 %copy.16 = f32[304,1,32]{0,2,1:T(8,128)} copy(f32[304,1,32]{0,2,1:T(8,128)} %bitcast.12) | data formatting | bytes 77824

commit v6 on v5

--- a/solution.py
+++ b/solution.py
@@ -441,46 +441,78 @@
 
     parents[...] = parents_of(windows[0, 1], child_ops)
     potentials[...] = jnp.zeros_like(potentials)
+    row = lax.broadcasted_iota(jnp.int32, (leaf_count, leaf_count), 0)
+
+    def one_hot(number, parts):
+        chosen = lists[number]
+        return jnp.concatenate(
+            [
+                jnp.where(row == chosen - part * leaf_count, 1.0, 0.0).astype(jnp.bfloat16)
+                for part in parts
+            ],
+            axis=0,
+        )
+
+    def gather(window, number, parts):
+        picked = jnp.dot(window, one_hot(number, parts), preferred_element_type=jnp.float32)
+        return picked.astype(jnp.bfloat16)
+
+    def place_of(offset):
+        return pl.ds(pl.multiple_of(offset * channels, 16), channels)
+
+    def operate(step):
+        pltpu.make_async_copy(
+            direct_in.at[:, pl.ds(0, width)], operators.at[step], operator_sem.at[step]
+        ).wait()
+        rows = pl.ds(pl.multiple_of(lax.rem(step, half) * width, 16), width)
+        potentials[...] += jnp.dot(
+            operators[step], gathered[rows, :], preferred_element_type=jnp.float32
+        )
+
+    def own_part(step, carry):
+        for o in range(batch // 2):
+            offset = step * (batch // 2) + o
+            gathered[place_of(offset), :] = gather(windows[0, 1], offset, (1,))
+        return carry
+
+    lax.fori_loop(0, 2 * half, own_part, 0)
     receive(direct)
-    row = lax.broadcasted_iota(jnp.int32, (leaf_count, leaf_count), 0)
-
-    def translate(step, carry):
+
+    def direct_step(step, carry):
         @pl.when(step == half // 2)
         def _():
             mirror.wait_recv()
             start(image)
 
-        @pl.when(step == half)
-        def _():
-            receive(image)
-
-        pltpu.make_async_copy(
-            direct_in.at[:, pl.ds(0, width)], operators.at[step], operator_sem.at[step]
-        ).wait()
-        slab = step // half
-        window = jnp.concatenate([windows[slab, part] for part in range(3)], axis=1)
+        window = jnp.concatenate([windows[0, 0], windows[0, 2]], axis=1)
         for o in range(batch):
-            chosen = lists[step * batch + o]
-            hot = jnp.concatenate(
-                [
-                    jnp.where(row == chosen - part * leaf_count, 1.0, 0.0).astype(jnp.bfloat16)
-                    for part in range(3)
-                ],
-                axis=0,
-            )
-            picked = jnp.dot(window, hot, preferred_element_type=jnp.float32)
-            gathered[pl.ds(o * channels, channels), :] = picked.astype(jnp.bfloat16)
-        potentials[...] += jnp.dot(
-            operators[step], gathered[...], preferred_element_type=jnp.float32
-        )
+            offset = step * batch + o
+            gathered[place_of(offset), :] += gather(window, offset, (0, 2))
+        operate(step)
         return carry
 
-    lax.fori_loop(0, steps, translate, 0)
+    lax.fori_loop(0, half, direct_step, 0)
+    receive(image)
+
+    def image_step(step, carry):
+        window = jnp.concatenate([windows[1, part] for part in range(3)], axis=1)
+        for o in range(batch):
+            offset = (step - half) * batch + o
+            gathered[place_of(offset), :] = gather(window, offsets + offset, (0, 1, 2))
+        operate(step)
+        return carry
+
+    lax.fori_loop(half, steps, image_step, 0)
     early_all.wait_send()
     late_all.wait_send()
     sent_off(direct)
     sent_off(image)
     mirror.wait_send()
+
+
+def hand_over_kernel(potentials, parents, potentials_out, parents_out):
+    potentials_out[:, 0, :] = potentials[...]
+    parents_out[...] = parents[...]
 
 
 def local(
@@ -538,7 +570,7 @@
             *[scratch(2 * part, blocks) for part in parts],
             *[scratch(devices, 1, width) for width in widths * 2],
             scratch(2, 3, channels, leaf_count, dtype=jnp.bfloat16),
-            scratch(batch * channels, leaf_count, dtype=jnp.bfloat16),
+            scratch(offsets * channels, leaf_count, dtype=jnp.bfloat16),
             pltpu.SemaphoreType.DMA((9,)),
             pltpu.SemaphoreType.DMA((steps,)),
             pltpu.SemaphoreType.DMA((2,)),
@@ -564,7 +596,17 @@
         direct_ops.T,
         image_ops.T,
     )
-    return (potentials[:, None, :], parents.T[:, None, :])
+    potentials, parents = pl.pallas_call(
+        hand_over_kernel,
+        out_shape=(
+            jax.ShapeDtypeStruct((channels, 1, leaf_count), jnp.float32),
+            jax.ShapeDtypeStruct((parent_count, channels), jnp.float32),
+        ),
+        in_specs=[VM, VM],
+        out_specs=(VM, VM),
+        name="hand_over",
+    )(potentials, parents)
+    return (potentials, parents.T[:, None, :])
 
 
 def solution(mesh):

time: 64 us -> 71.3 us (1.11)
  Pallas kernels: 59.7 us -> 70.5 us
  local copies, waits for them, and re-layouts: 3.43 us -> 0 us
    pallas_call x1, Pallas kernels: 59.7 us -> 68.7 us  [local(): pl.pallas_call(step_kernel, out_shape=(jax.ShapeDtypeStruct((channels, le...]
    unnamed x2 -> x0, local copies, waits for them, and re-layouts: 3.43 us -> none
    pallas_call x0 -> x1, Pallas kernels: none -> 1.78 us  [local(): pl.pallas_call(hand_over_kernel, out_shape=(jax.ShapeDtypeStruct((channel...]
where the time goes in v6:
time: 71.3 us; the launch traced here: 71.1 us
  Pallas kernels  70.5 us (99%)
    pallas_call x1, Pallas kernels, local(): pl.pallas_call(step_kernel, out_shape=(jax.ShapeDtypeStruct((channels, le...  68.7 us
    pallas_call x1, Pallas kernels, local(): pl.pallas_call(hand_over_kernel, out_shape=(jax.ShapeDtypeStruct((channel...  1.78 us

profile of v6, /device:TPU:1, one launch (start us, length us, event | category | flops | bytes accessed | tf_op | source)
XLA Modules:
  0.0 71.1 jit_solution(6356486341423941410)
XLA Ops:
  0.6 68.7 %step.1 = (f32[304,256]{1,0:T(8,128)}, f32[32,304]{1,0:T(8,128)}) custom-call(s32[2,152]{1,0:T(2,128)} %constant.2.clone.table, f32[3,128,128]{2,1,0:T(8,128)} %positions_in.1, f32[2,128,128]{2,1,0:T(8,128)} %charges_in.1, s32[1,128]{1,0:T(1,128)} %bitcast.10, s32[1,128]{1,0:T(1,128)} %bitcast.11, s32[1,128]{1,0:T(1,128)} %bitcast.12, ...), custom_call_target="tpu_custom_call" | custom-call | tf_op jit(solution)/shard_map/step/pallas_call | solution.py:549
  69.3 1.8 %hand_over.1 = (f32[304,1,256]{2,1,0:T(1,128)}, f32[32,304]{1,0:T(8,128)}) custom-call(f32[304,256]{1,0:T(8,128)} %get-tuple-element.6.potentials, f32[32,304]{1,0:T(8,128)} %get-tuple-element.7.parents), custom_call_target="tpu_custom_call" | custom-call | tf_op jit(solution)/shard_map/hand_over/pallas_call | solution.py:599

commit v7 on v5

--- a/solution.py
+++ b/solution.py
@@ -427,7 +427,6 @@
             pair[1].wait_send()
 
     start(direct)
-    mirror.start()
 
     @pl.when(jnp.logical_not(has_left))
     def _():
@@ -442,6 +441,7 @@
     parents[...] = parents_of(windows[0, 1], child_ops)
     potentials[...] = jnp.zeros_like(potentials)
     receive(direct)
+    mirror.start()
     row = lax.broadcasted_iota(jnp.int32, (leaf_count, leaf_count), 0)
 
     def translate(step, carry):
@@ -481,6 +481,11 @@
     sent_off(direct)
     sent_off(image)
     mirror.wait_send()
+
+
+def hand_over_kernel(potentials, parents, potentials_out, parents_out):
+    potentials_out[:, 0, :] = potentials[...]
+    parents_out[...] = parents[...]
 
 
 def local(
@@ -564,7 +569,17 @@
         direct_ops.T,
         image_ops.T,
     )
-    return (potentials[:, None, :], parents.T[:, None, :])
+    potentials, parents = pl.pallas_call(
+        hand_over_kernel,
+        out_shape=(
+            jax.ShapeDtypeStruct((channels, 1, leaf_count), jnp.float32),
+            jax.ShapeDtypeStruct((parent_count, channels), jnp.float32),
+        ),
+        in_specs=[VM, VM],
+        out_specs=(VM, VM),
+        name="hand_over",
+    )(potentials, parents)
+    return (potentials, parents.T[:, None, :])
 
 
 def solution(mesh):

time: 64 us -> 61.9 us (0.967)
  local copies, waits for them, and re-layouts: 3.43 us -> 0 us
  Pallas kernels: 59.7 us -> 60.7 us
    unnamed x2 -> x0, local copies, waits for them, and re-layouts: 3.43 us -> none
    pallas_call x0 -> x1, Pallas kernels: none -> 1.78 us  [local(): pl.pallas_call(hand_over_kernel, out_shape=(jax.ShapeDtypeStruct((channel...]
    pallas_call x1, Pallas kernels: 59.7 us -> 58.9 us  [local(): pl.pallas_call(step_kernel, out_shape=(jax.ShapeDtypeStruct((channels, le...]
where the time goes in v7:
time: 61.9 us; the launch traced here: 61.3 us
  Pallas kernels  60.7 us (98%)
  between operations  0.64 us (1%)
    pallas_call x1, Pallas kernels, local(): pl.pallas_call(step_kernel, out_shape=(jax.ShapeDtypeStruct((channels, le...  58.9 us
    pallas_call x1, Pallas kernels, local(): pl.pallas_call(hand_over_kernel, out_shape=(jax.ShapeDtypeStruct((channel...  1.78 us

profile of v7, /device:TPU:1, one launch (start us, length us, event | category | flops | bytes accessed | tf_op | source)
XLA Modules:
  0.0 61.3 jit_solution(16219833318896055336)
XLA Ops:
  0.6 58.9 %step.1 = (f32[304,256]{1,0:T(8,128)}, f32[32,304]{1,0:T(8,128)}) custom-call(s32[2,152]{1,0:T(2,128)} %constant.2.clone.table, f32[3,128,128]{2,1,0:T(8,128)} %positions_in.1, f32[2,128,128]{2,1,0:T(8,128)} %charges_in.1, s32[1,128]{1,0:T(1,128)} %bitcast.10, s32[1,128]{1,0:T(1,128)} %bitcast.11, s32[1,128]{1,0:T(1,128)} %bitcast.12, ...), custom_call_target="tpu_custom_call" | custom-call | tf_op jit(solution)/shard_map/step/pallas_call | solution.py:522
  59.6 1.8 %hand_over.1 = (f32[304,1,256]{2,1,0:T(1,128)}, f32[32,304]{1,0:T(8,128)}) custom-call(f32[304,256]{1,0:T(8,128)} %get-tuple-element.6.potentials, f32[32,304]{1,0:T(8,128)} %get-tuple-element.7.parents), custom_call_target="tpu_custom_call" | custom-call | tf_op jit(solution)/shard_map/hand_over/pallas_call | solution.py:572

commit v8 on v7

--- a/solution.py
+++ b/solution.py
@@ -232,6 +232,7 @@
     late_arrived,
     windows,
     gathered,
+    own_gathered,
     input_sem,
     operator_sem,
     send_sem,
@@ -317,7 +318,7 @@
         sum_point(table, planes, depths, live_charges, early_values, 0, p)
         return carry
 
-    lax.fori_loop(0, early, early_point, 0, unroll=4)
+    lax.fori_loop(0, early, early_point, 0, unroll=8)
     fill_slots(early_values, owners, rank, leaves, early_sent, capacity)
     pl.semaphore_wait(barrier, devices - 1)
 
@@ -350,22 +351,25 @@
     early_all = all_routed(0, early_sent, early_arrived)
     late_all = all_routed(1, late_sent, late_arrived)
     own_row(early_send)
-
-    def late_points(pair):
-        for p in range(2):
-            sum_point(table, planes, depths, live_charges, late_values, early, 2 * pair + p)
-
-    def late_and_send(pair, carry):
-        late_points(pair)
-        one_row(pair + 1, early_send)
+    one_row(boxes - 1, early_send)
+
+    def late_points(group):
+        for p in range(4):
+            sum_point(table, planes, depths, live_charges, late_values, early, 4 * group + p)
+
+    def late_and_send(group, carry):
+        late_points(group)
+        for ahead in range(2):
+            one_row(2 * group + 1 + ahead, early_send)
         return carry
 
-    def late_only(pair, carry):
-        late_points(pair)
+    def late_only(group, carry):
+        late_points(group)
         return carry
 
-    lax.fori_loop(0, boxes - 1, late_and_send, 0)
-    lax.fori_loop(boxes - 1, late // 2, late_only, 0)
+    sending = (boxes - 2) // 2
+    lax.fori_loop(0, sending, late_and_send, 0)
+    lax.fori_loop(sending, late // 4, late_only, 0)
     fill_slots(late_values, owners, rank, leaves, late_sent, capacity)
     own_row(late_send)
     other_rows(late_send)
@@ -439,10 +443,32 @@
         windows[1, 2] = blank
 
     parents[...] = parents_of(windows[0, 1], child_ops)
-    potentials[...] = jnp.zeros_like(potentials)
+    row = lax.broadcasted_iota(jnp.int32, (leaf_count, leaf_count), 0)
+
+    def gather(window, number, parts):
+        chosen = lists[number]
+        hot = jnp.concatenate(
+            [
+                jnp.where(row == chosen - part * leaf_count, 1.0, 0.0).astype(jnp.bfloat16)
+                for part in parts
+            ],
+            axis=0,
+        )
+        return jnp.dot(window, hot, preferred_element_type=jnp.float32).astype(jnp.bfloat16)
+
+    own = windows[0, 1]
+    for o in range(batch):
+        own_gathered[pl.ds(o * channels, channels), :] = gather(own, o, (1,))
     receive(direct)
     mirror.start()
-    row = lax.broadcasted_iota(jnp.int32, (leaf_count, leaf_count), 0)
+    beside_own = jnp.concatenate([windows[0, 0], windows[0, 2]], axis=1)
+    for o in range(batch):
+        place = pl.ds(o * channels, channels)
+        gathered[place, :] = own_gathered[place, :] + gather(beside_own, o, (0, 2))
+    pltpu.make_async_copy(
+        direct_in.at[:, pl.ds(0, width)], operators.at[0], operator_sem.at[0]
+    ).wait()
+    potentials[...] = jnp.dot(operators[0], gathered[...], preferred_element_type=jnp.float32)
 
     def translate(step, carry):
         @pl.when(step == half // 2)
@@ -460,22 +486,15 @@
         slab = step // half
         window = jnp.concatenate([windows[slab, part] for part in range(3)], axis=1)
         for o in range(batch):
-            chosen = lists[step * batch + o]
-            hot = jnp.concatenate(
-                [
-                    jnp.where(row == chosen - part * leaf_count, 1.0, 0.0).astype(jnp.bfloat16)
-                    for part in range(3)
-                ],
-                axis=0,
+            gathered[pl.ds(o * channels, channels), :] = gather(
+                window, step * batch + o, (0, 1, 2)
             )
-            picked = jnp.dot(window, hot, preferred_element_type=jnp.float32)
-            gathered[pl.ds(o * channels, channels), :] = picked.astype(jnp.bfloat16)
         potentials[...] += jnp.dot(
             operators[step], gathered[...], preferred_element_type=jnp.float32
         )
         return carry
 
-    lax.fori_loop(0, steps, translate, 0)
+    lax.fori_loop(1, steps, translate, 0)
     early_all.wait_send()
     late_all.wait_send()
     sent_off(direct)
@@ -544,6 +563,7 @@
             *[scratch(devices, 1, width) for width in widths * 2],
             scratch(2, 3, channels, leaf_count, dtype=jnp.bfloat16),
             scratch(batch * channels, leaf_count, dtype=jnp.bfloat16),
+            scratch(batch * channels, leaf_count, dtype=jnp.bfloat16),
             pltpu.SemaphoreType.DMA((9,)),
             pltpu.SemaphoreType.DMA((steps,)),
             pltpu.SemaphoreType.DMA((2,)),

time: 61.9 us -> 60.5 us (0.977)
  Pallas kernels: 60.7 us -> 59.7 us
    pallas_call x1, Pallas kernels: 58.9 us -> 57.9 us  [local(): pl.pallas_call(step_kernel, out_shape=(jax.ShapeDtypeStruct((channels, le...]
where the time goes in v8:
time: 60.5 us; the launch traced here: 60.3 us
  Pallas kernels  59.7 us (99%)
  between operations  0.64 us (1%)
    pallas_call x1, Pallas kernels, local(): pl.pallas_call(step_kernel, out_shape=(jax.ShapeDtypeStruct((channels, le...  57.9 us
    pallas_call x1, Pallas kernels, local(): pl.pallas_call(hand_over_kernel, out_shape=(jax.ShapeDtypeStruct((channel...  1.78 us

profile of v8, /device:TPU:1, one launch (start us, length us, event | category | flops | bytes accessed | tf_op | source)
XLA Modules:
  0.0 60.3 jit_solution(10837646538100248982)
XLA Ops:
  0.6 57.9 %step.1 = (f32[304,256]{1,0:T(8,128)}, f32[32,304]{1,0:T(8,128)}) custom-call(s32[2,152]{1,0:T(2,128)} %constant.2.clone.table, f32[3,128,128]{2,1,0:T(8,128)} %positions_in.1, f32[2,128,128]{2,1,0:T(8,128)} %charges_in.1, s32[1,128]{1,0:T(1,128)} %bitcast.10, s32[1,128]{1,0:T(1,128)} %bitcast.11, s32[1,128]{1,0:T(1,128)} %bitcast.12, ...), custom_call_target="tpu_custom_call" | custom-call | tf_op jit(solution)/shard_map/step/pallas_call | solution.py:541
  58.6 1.8 %hand_over.1 = (f32[304,1,256]{2,1,0:T(1,128)}, f32[32,304]{1,0:T(8,128)}) custom-call(f32[304,256]{1,0:T(8,128)} %get-tuple-element.6.potentials, f32[32,304]{1,0:T(8,128)} %get-tuple-element.7.parents), custom_call_target="tpu_custom_call" | custom-call | tf_op jit(solution)/shard_map/hand_over/pallas_call | solution.py:592

commit v9 on v8

--- a/solution.py
+++ b/solution.py
@@ -444,12 +444,14 @@
 
     parents[...] = parents_of(windows[0, 1], child_ops)
     row = lax.broadcasted_iota(jnp.int32, (leaf_count, leaf_count), 0)
+    row = row.astype(jnp.float32).astype(jnp.bfloat16)
+    hit, miss = jnp.ones((), jnp.bfloat16), jnp.zeros((), jnp.bfloat16)
 
     def gather(window, number, parts):
-        chosen = lists[number]
+        chosen = lists[number].astype(jnp.float32)
         hot = jnp.concatenate(
             [
-                jnp.where(row == chosen - part * leaf_count, 1.0, 0.0).astype(jnp.bfloat16)
+                jnp.where(row == (chosen - float(part * leaf_count)).astype(jnp.bfloat16), hit, miss)
                 for part in parts
             ],
             axis=0,
@@ -530,7 +532,7 @@
     batch = 32
     steps = 2 * offsets // batch
     points = channels // 2
-    early = points * 11 // 16 // 8 * 8
+    early = points * 13 // 16 // 8 * 8
     parts = (early, points - early)
     widths = [-(-capacity * (2 * part + 1) // 128) * 128 for part in parts]
     parent_count = leaf_count * channels // child_ops.shape[1]

time: 60.5 us -> 59.9 us (0.990)
  no operation moved by 1% of the time
where the time goes in v9:
time: 59.9 us; the launch traced here: 59.8 us
  Pallas kernels  59.1 us (99%)
  between operations  0.64 us (1%)
    pallas_call x1, Pallas kernels, local(): pl.pallas_call(step_kernel, out_shape=(jax.ShapeDtypeStruct((channels, le...  57.3 us
    pallas_call x1, Pallas kernels, local(): pl.pallas_call(hand_over_kernel, out_shape=(jax.ShapeDtypeStruct((channel...  1.78 us

profile of v9, /device:TPU:1, one launch (start us, length us, event | category | flops | bytes accessed | tf_op | source)
XLA Modules:
  0.0 59.8 jit_solution(5738380491163186923)
XLA Ops:
  0.6 57.3 %step.1 = (f32[304,256]{1,0:T(8,128)}, f32[32,304]{1,0:T(8,128)}) custom-call(s32[2,152]{1,0:T(2,128)} %constant.2.clone.table, f32[3,128,128]{2,1,0:T(8,128)} %positions_in.1, f32[2,128,128]{2,1,0:T(8,128)} %charges_in.1, s32[1,128]{1,0:T(1,128)} %bitcast.10, s32[1,128]{1,0:T(1,128)} %bitcast.11, s32[1,128]{1,0:T(1,128)} %bitcast.12, ...), custom_call_target="tpu_custom_call" | custom-call | tf_op jit(solution)/shard_map/step/pallas_call | solution.py:543
  58.0 1.8 %hand_over.1 = (f32[304,1,256]{2,1,0:T(1,128)}, f32[32,304]{1,0:T(8,128)}) custom-call(f32[304,256]{1,0:T(8,128)} %get-tuple-element.6.potentials, f32[32,304]{1,0:T(8,128)} %get-tuple-element.7.parents), custom_call_target="tpu_custom_call" | custom-call | tf_op jit(solution)/shard_map/hand_over/pallas_call | solution.py:594
